TPU v7x, 128 devices: a whole 4x4x4 slice. The times are simulated.
128 devices in a mesh: region: 32 (over x, z, core), basis: 4 (over y).
Axes of the slice: x: 4, y: 4, z: 4, core: 2. Of those that a mesh axis runs over, the one named last changes fastest.
Arguments:
- observations: bfloat16 [1048576, 128], P(('region', 'basis')), may hold values from -3 to 4
- basis_values: bfloat16 [1048576, 1024], P(('region', 'basis')), as said below
- mixing: bfloat16 [1024, 1024], P('basis'), may hold values from -0.1875 to 0.1875
- pattern: int32 [8, 8], replicated, may hold values 0 or 1
- decays: float32 [32, 1024], P('region', 'basis'), may hold values from 0 to 1
- loadings: float32 [1024], P('basis'), may hold values from 0.3 to 3
Outputs:
- obs_grad: bfloat16 [1048576, 128], P(('region', 'basis'))
- attenuation_slope: float32 [32, 1024], P('region', 'basis')
Inputs may be any that keep to these rules, and one draw needn't show every extreme that they name: `basis_values`: every entry lies within 3.5 / 32768 ** 0.5 of zero.
All inputs are finite; a program needn't handle non-finite values.
Results may differ from a plain program's by a relative error of at most 0.015.
Values may be sent and summed in bfloat16 or wider, within the bound.
No kernel may reach another device: no remote copies, remote signals or barrier semaphores. Data moves between devices by JAX's collectives and lax.ppermute only.
A program may use at most 128 MiB of HBM per device.

v0:
```python
import jax
import jax.numpy as jnp
from jax import lax
from jax.sharding import PartitionSpec as P

BLOCK = 128


def entering(value, axis, join, neutral, backward):
    count, mine = (lax.axis_size(axis), lax.axis_index(axis))
    pieces = jax.tree.map(lambda part: lax.all_gather(part, axis), value)
    if backward:
        pieces = jax.tree.map(lambda part: part[::-1], pieces)
        mine = count - 1 - mine
    subtotal = jax.tree.map(
        lambda part, zero: jnp.full_like(part, 0) + jnp.asarray(zero, part.dtype), value, neutral
    )

    def turn(position, subtotal):
        longer = join(subtotal, jax.tree.map(lambda part: part[position], pieces))
        return jax.tree.map(lambda new, old: jnp.where(position < mine, new, old), longer, subtotal)

    return lax.fori_loop(0, count - 1, turn, subtotal)


def contract_rows(first_operand, second_operand):
    return lax.dot_general(
        first_operand, second_operand, (((0,), (0,)), ((), ())), preferred_element_type=jnp.float32
    )


def block_rows(mixing, pattern, owner):
    row_count = mixing.shape[0]
    width = mixing.shape[1]
    row_ids = owner * row_count + jnp.arange(row_count)
    column_index = jnp.arange(width)
    labels = jnp.arange(pattern.shape[0])
    row_hot = ((row_ids // BLOCK)[:, None] == labels[None, :]).astype(jnp.float32)
    column_hot = ((column_index // BLOCK)[:, None] == labels[None, :]).astype(jnp.float32)
    expanded = jnp.dot(jnp.dot(row_hot, pattern.astype(jnp.float32)), column_hot.T)
    identity = (row_ids[:, None] == column_index[None, :]).astype(jnp.float32)
    return (identity + mixing.astype(jnp.float32) * expanded).astype(jnp.bfloat16)


def combine(earlier, later):
    return (earlier[0] * later[0], later[0][:, None] * earlier[1] + later[1])


def shards(observations, basis_values, mixing, pattern, decays, loadings):
    owner = lax.axis_index("basis")
    share = mixing.shape[0]
    characteristics = observations.shape[1]
    mixer_rows = block_rows(mixing, pattern, owner)
    rates = decays[0]
    zero_share = jnp.zeros((share, characteristics), jnp.float32)
    identity_pair = (jnp.ones((share,), jnp.float32), zero_share)

    def predict_piece(piece):
        return jnp.dot(basis_values, piece, preferred_element_type=jnp.float32)

    summary = lax.psum_scatter(
        contract_rows(basis_values, observations), "basis", scatter_dimension=0, tiled=True
    )
    mixed_terms = jnp.dot(
        mixer_rows,
        lax.all_gather(summary.astype(jnp.bfloat16), "basis", axis=0, tiled=True),
        preferred_element_type=jnp.float32,
    )
    _, previous = entering((rates, mixed_terms), "region", combine, identity_pair, False)
    states = rates[:, None] * previous + mixed_terms
    loaded_values = (loadings[:, None] * states).astype(jnp.bfloat16)
    fitted = predict_piece(lax.all_gather(loaded_values, "basis", axis=0, tiled=True))
    residual = (fitted - observations.astype(jnp.float32)).astype(jnp.bfloat16)
    pulled = loadings[:, None] * lax.psum_scatter(
        contract_rows(basis_values, residual).astype(jnp.bfloat16),
        "basis",
        scatter_dimension=0,
        tiled=True,
    ).astype(jnp.float32)
    _, carried = entering((rates, rates[:, None] * pulled), "region", combine, identity_pair, True)
    adjoints = pulled + carried
    attenuation_slope = (jnp.sum(adjoints * previous, axis=1) / characteristics)[None, :]
    adjoint_b = adjoints.astype(jnp.bfloat16)
    back_owned = lax.psum_scatter(
        contract_rows(mixer_rows, adjoint_b), "basis", scatter_dimension=0, tiled=True
    ).astype(jnp.bfloat16)
    spread = predict_piece(lax.all_gather(back_owned, "basis", axis=0, tiled=True))
    obs_grad = (spread - residual.astype(jnp.float32)).astype(jnp.bfloat16)
    return (obs_grad, attenuation_slope)


def solution(mesh):
    in_specs = (
        P(("region", "basis"), None),
        P(("region", "basis"), None),
        P("basis", None),
        P(),
        P("region", "basis"),
        P("basis"),
    )
    out_specs = (P(("region", "basis"), None), P("region", "basis"))
    return jax.shard_map(shards, mesh=mesh, in_specs=in_specs, out_specs=out_specs, check_vma=False)
```

profile of v0, /device:TPU:1, one launch (start us, length us, event | category | flops | bytes accessed | tf_op | source)
XLA Modules:
  0.0 334.5 jit_solution(7736925620875022976)
XLA Ops:
  7.2 11.7 %fusion.25 = f32[1024,128]{1,0:T(8,128)} fusion(bf16[8192,1024]{1,0:T(8,128)(2,1)} %param.11, bf16[8192,128]{1,0:T(8,128)(2,1)} %param.10), kind=kOutput, calls=%fused_computation.46 | convolution fusion | flops 2147483648 | bytes 19398656 | tf_op jit(solution)/shard_map/dot_general | solution.py:27
  19.0 1.7 fusion.7
  20.7 21.3 %reduce-scatter.4.cloned.1.call-done = f32[256,128]{1,0:T(8,128)} async-done(((f32[1024,128]{1,0:T(8,128)}), f32[256,128]{1,0:T(8,128)}) %reduce-scatter.4.cloned.1.call-update) | async-done | bytes 131088 | tf_op jit(solution)/shard_map/reduce_scatter | solution.py:61
  43.0 9.7 %all_gather.26 = bf16[1024,128]{1,0:T(8,128)(2,1)S(1)} all-gather(bf16[256,128]{1,0:T(8,128)(2,1)S(1)} %convert_element_type.51), channel_id=1, replica_groups=mesh['region'=32,'basis'=4] {'basis'}, dimensions={0}, use_global_device_ids=true | all-gather | bytes 327680 | tf_op jit(solution)/shard_map/all_gather | solution.py:66
  53.7 2.9 copy.11
  56.6 29.1 %all-gather.2 = f32[32,1,256]{2,1,0:T(1,128)S(1)} all-gather(f32[1,1,256]{2,1,0:T(1,128)S(1)} %bitcast.56), channel_id=1, replica_groups=mesh['region'=32,'basis'=4] {'region'}, dimensions={0}, use_global_device_ids=true | all-gather | bytes 33792 | tf_op jit(solution)/shard_map/all_gather | solution.py:11
  85.6 18.9 %all-gather.6.cloned.1.call-done = f32[8192,128]{1,0:T(8,128)} async-done(((f32[256,128]{1,0:T(8,128)}), f32[8192,128]{1,0:T(8,128)}) %all-gather.6.cloned.1.call-update) | async-done | bytes 4194320 | tf_op jit(solution)/shard_map/all_gather | solution.py:11
  104.5 33.2 %while.28 = (s32[]{:T(128)}, f32[256,128]{1,0:T(8,128)S(1)}, s32[]{:T(128)}, f32[32,256]{1,0:T(8,128)S(1)}, f32[32,256,128]{2,1,0:T(8,128)}, /*index=5*/s32[]{:T(128)}, s32[]{:T(128)}) while((s32[]{:T(128)}, f32[256,128]{1,0:T(8,128)S(1)}, s32[]{:T(128)}, f32[32,256]{1,0:T(8,128)S(1)}, f32[32,256,128]{2,1,0:T(8,128)}, ...), condition=%wide.region_2.3_spmd.clone, body=%wide.region_1.2_spmd.clone.sunk | while | flops 131076 | bytes 396393 | solution.py:23
  105.6 1.0 fusion.40
  106.7 1.0 fusion.40
  107.8 1.0 fusion.40
  108.8 1.0 fusion.40
  109.9 1.0 fusion.40
  111.0 1.0 fusion.40
  112.0 1.0 fusion.40
  116.3 1.0 fusion.40
  136.7 1.0 fusion.40
  137.9 10.5 %all_gather.29 = bf16[1024,128]{1,0:T(8,128)(2,1)S(1)} all-gather(bf16[256,128]{1,0:T(8,128)(2,1)S(1)} %multiply_convert_fusion), channel_id=1, replica_groups=mesh['region'=32,'basis'=4] {'basis'}, dimensions={0}, use_global_device_ids=true | all-gather | bytes 327680 | tf_op jit(solution)/shard_map/all_gather | solution.py:72
  148.4 12.0 %fusion.5 = bf16[8192,128]{0,1:T(8,128)(2,1)S(1)} fusion(bf16[1024,128]{1,0:T(8,128)(2,1)S(1)} %all_gather.29, bf16[8192,1024]{1,0:T(8,128)(2,1)} %param.11, bf16[8192,128]{0,1:T(8,128)(2,1)} %copy.11), kind=kOutput, calls=%fused_computation.11 | convolution fusion | flops 2150629376 | bytes 21233664 | tf_op jit(solution)/shard_map/dot_general | solution.py:59
  160.4 10.8 %fusion.8 = bf16[1024,128]{1,0:T(8,128)(2,1)} fusion(bf16[8192,128]{0,1:T(8,128)(2,1)S(1)} %fusion.5, bf16[8192,1024]{1,0:T(8,128)(2,1)} %param.11), kind=kOutput, calls=%fused_computation.16 | convolution fusion | flops 2147614720 | bytes 19136512 | tf_op jit(solution)/shard_map/dot_general | solution.py:27
  171.3 19.3 %reduce-scatter.6.cloned.1.call-done = bf16[256,128]{1,0:T(8,128)(2,1)} async-done(((bf16[1024,128]{1,0:T(8,128)(2,1)}), bf16[256,128]{1,0:T(8,128)(2,1)}) %reduce-scatter.6.cloned.1.call-update) | async-done | bytes 65552 | tf_op jit(solution)/shard_map/reduce_scatter | solution.py:74
  190.7 1.6 fusion.13
  192.5 49.9 %all-gather.8.cloned.1.call-done = f32[8192,128]{1,0:T(8,128)} async-done(((f32[256,128]{1,0:T(8,128)}), f32[8192,128]{1,0:T(8,128)}) %all-gather.8.cloned.1.call-update) | async-done | bytes 4194320 | tf_op jit(solution)/shard_map/all_gather | solution.py:11
  242.4 4.6 %rev.7 = f32[32,256,128]{2,1,0:T(8,128)} reverse(f32[32,256,128]{2,1,0:T(8,128)} %bitcast.51), dimensions={0} | reverse | bytes 8388608 | tf_op jit(solution)/shard_map/rev | solution.py:13
  247.0 33.2 %while.29 = (s32[]{:T(128)}, f32[256,128]{1,0:T(8,128)S(1)}, s32[]{:T(128)}, f32[32,256]{1,0:T(8,128)S(1)}, f32[32,256,128]{2,1,0:T(8,128)}, /*index=5*/s32[]{:T(128)}, s32[]{:T(128)}) while((s32[]{:T(128)}, f32[256,128]{1,0:T(8,128)S(1)}, s32[]{:T(128)}, f32[32,256]{1,0:T(8,128)S(1)}, f32[32,256,128]{2,1,0:T(8,128)}, ...), condition=%wide.region_5.6_spmd.clone, body=%wide.region_4.5_spmd.clone.sunk | while | flops 131076 | bytes 396393 | solution.py:23
  257.7 1.0 fusion.41
  278.1 1.0 fusion.41
  280.2 1.2 fusion.15
  282.2 18.0 %reduce-scatter.8.cloned.1.call-done = f32[256,128]{1,0:T(8,128)} async-done(((f32[1024,128]{1,0:T(8,128)}), f32[256,128]{1,0:T(8,128)}) %reduce-scatter.8.cloned.1.call-update) | async-done | bytes 131088 | tf_op jit(solution)/shard_map/reduce_scatter | solution.py:84
  301.2 9.9 %all_gather.32 = bf16[1024,128]{1,0:T(8,128)(2,1)S(1)} all-gather(bf16[256,128]{1,0:T(8,128)(2,1)S(1)} %convert_element_type.59), channel_id=1, replica_groups=mesh['region'=32,'basis'=4] {'basis'}, dimensions={0}, use_global_device_ids=true | all-gather | bytes 327680 | tf_op jit(solution)/shard_map/all_gather | solution.py:87
  311.1 12.8 %fusion.4 = bf16[8192,128]{0,1:T(8,128)(2,1)} fusion(bf16[1024,128]{1,0:T(8,128)(2,1)S(1)} %all_gather.32, bf16[8192,1024]{1,0:T(8,128)(2,1)} %param.11, bf16[8192,128]{0,1:T(8,128)(2,1)S(1)} %fusion.5), kind=kOutput, calls=%fused_computation.10 | convolution fusion | flops 2150629376 | bytes 21233664 | tf_op jit(solution)/shard_map/dot_general | solution.py:59
  323.9 4.1 %copy.13 = bf16[8192,128]{1,0:T(8,128)(2,1)} copy(bf16[8192,128]{0,1:T(8,128)(2,1)} %fusion.4) | data formatting | bytes 4194304
  (147 shorter events, 57.1 us)
Async XLA Ops:
  7.2 11.8 %copy-start.5 = (s32[8,8]{1,0:T(8,128)S(1)}, s32[8,8]{1,0:T(8,128)}, u32[]{:S(2)}) copy-start(s32[8,8]{1,0:T(8,128)} %param.13) | copy-start | bytes 772
  7.2 34.9 %reduce-scatter.4.cloned.1.call-start = ((), (), s32[]{:S(2)}) async-start(), calls=%async_computation.3 | async-start | bytes 655360 | tf_op jit(solution)/shard_map/reduce_scatter | solution.py:61
  18.9 34.8 %copy-start = (bf16[8192,128]{1,0:T(8,128)(2,1)S(1)}, bf16[8192,128]{1,0:T(8,128)(2,1)}, u32[]{:S(2)}) copy-start(bf16[8192,128]{1,0:T(8,128)(2,1)} %param.10) | copy-start | bytes 6291460
  18.9 37.7 %copy-start.4 = (f32[1,256]{1,0:T(1,128)S(1)}, f32[1,256]{1,0:T(1,128)}, u32[]{:S(2)}) copy-start(f32[1,256]{1,0:T(1,128)} %param.14) | copy-start | bytes 3076
  18.9 85.6 %all-gather.6.cloned.1.call-start = ((), (), s32[]{:S(2)}) async-start(), calls=%async_computation.6 | async-start | bytes 4325376 | tf_op jit(solution)/shard_map/all_gather | solution.py:11
  20.7 117.0 %copy-start.3 = (f32[256]{0:T(256)S(1)}, f32[256]{0:T(256)}, u32[]{:S(2)}) copy-start(f32[256]{0:T(256)} %param.15) | copy-start | bytes 3076
  53.6 84.2 %copy-start.1 = (f32[256,128]{1,0:T(8,128)S(1)}, f32[256,128]{1,0:T(8,128)}, u32[]{:S(2)}) copy-start(f32[256,128]{1,0:T(8,128)} %fusion.26) | copy-start | bytes 393220
  53.6 137.1 %reduce-scatter.6.cloned.1.call-start = ((), (), s32[]{:S(2)}) async-start(), calls=%async_computation.4 | async-start | bytes 327680 | tf_op jit(solution)/shard_map/reduce_scatter | solution.py:74
  171.3 71.1 %all-gather.8.cloned.1.call-start = ((), (), s32[]{:S(2)}) async-start(), calls=%async_computation.7 | async-start | bytes 4325376 | tf_op jit(solution)/shard_map/all_gather | solution.py:11
  192.3 107.9 %reduce-scatter.8.cloned.1.call-start = ((), (), s32[]{:S(2)}) async-start(), calls=%async_computation.5 | async-start | bytes 655360 | tf_op jit(solution)/shard_map/reduce_scatter | solution.py:84
  242.4 37.8 %copy-start.2 = (bf16[256,128]{1,0:T(8,128)(2,1)S(1)}, bf16[256,128]{1,0:T(8,128)(2,1)}, u32[]{:S(2)}) copy-start(bf16[256,128]{1,0:T(8,128)(2,1)} %reduce-scatter.6.cloned.1.call-done) | copy-start | bytes 196612
Sparse Core Ops, SparseCore 0:
  19.0 22.9 reduce-scatter.3
  53.7 50.7 all-gather.5
  171.4 19.2 reduce-scatter.5
  193.6 48.7 all-gather.7
  281.6 18.6 reduce-scatter.7
where the time goes:
time: 339 us; the launch traced here: 334 us
  waiting for transfers between devices  128 us (38%)
  other arithmetic  68.1 us (20%)
  blocking collectives  59.2 us (17%)
  matrix products  51.1 us (15%)
  between operations  13.9 us (4%)
  local copies, waits for them, and re-layouts  12.3 us (4%)
    all_gather x2, waiting for transfers between devices, entering(): pieces = jax.tree.map(lambda part: lax.all_gather(part, axis), value)  68.8 us
    select_n x62, other arithmetic, turn(): jnp.where(position < mine, new, old)  63.8 us
    all_gather x1, blocking collectives, entering(): pieces = jax.tree.map(lambda part: lax.all_gather(part, axis), value)  29.1 us
    dot_general x2, matrix products, predict_piece(): return jnp.dot(basis_values, piece, preferred_element_type=jnp.float32)  24.8 us
    dot_general x3, matrix products, contract_rows(): lax.dot_general(first_operand, second_operand, (((0,), (0,)), ((), ())),...  23.7 us
    reduce_scatter x1, waiting for transfers between devices, shards(): lax.psum_scatter(contract_rows(basis_values, observations), 'basis', scat...  21.3 us
    reduce_scatter x1, waiting for transfers between devices, shards(): lax.psum_scatter(contract_rows(basis_values, residual).astype(jnp.bfloat1...  19.3 us
    reduce_scatter x1, waiting for transfers between devices, shards(): lax.psum_scatter(contract_rows(mixer_rows, adjoint_b), 'basis', scatter_d...  18 us
  transfers between devices with their start and end apart: 5, of which 5 were waited for; matrix products, arithmetic and copies ran while one was open for 2% of the time, Pallas kernels for 0%

commit v1 on v0

v1 whole, which is shorter than its diff:
```python
import functools

import jax
import jax.numpy as jnp
from jax import lax
from jax.experimental import pallas as pl
from jax.experimental.pallas import tpu as pltpu
from jax.sharding import PartitionSpec as P

BLOCK = 128
LANES = 128
TILE_ROWS = 1024
VMEM_LIMIT = 56 * 1024 * 1024
ALL = ("region", "basis")
F32 = jnp.float32
BF16 = jnp.bfloat16


def split(value):
    high = value.astype(BF16)
    return high, (value - high.astype(F32)).astype(BF16)


def compiler_params():
    return pltpu.CompilerParams(
        dimension_semantics=("arbitrary",), vmem_limit_bytes=VMEM_LIMIT
    )


def contract_rows(first, second):
    return lax.dot_general(first, second, (((0,), (0,)), ((), ())), preferred_element_type=F32)


def contract_lanes(first, second):
    return lax.dot_general(first, second, (((1,), (1,)), ((), ())), preferred_element_type=F32)


def store_by_trait(total, spread, message):
    traits, width = total.shape
    groups = width // LANES
    for s in range(groups):
        spread[pl.ds(s, traits, stride=groups), :] = total[:, s * LANES : (s + 1) * LANES]
    message[:, 0:groups, :] = spread[...].reshape(traits, groups, LANES).astype(BF16)


def load_by_trait(message, spread, target, at):
    traits = message.shape[0]
    groups = target.shape[1] // LANES
    spread[...] = message[:, 0:groups, :].astype(F32).reshape(traits * groups, LANES)
    for s in range(groups):
        target[at : at + traits, s * LANES : (s + 1) * LANES] = spread[
            pl.ds(s, traits, stride=groups), :
        ].astype(BF16)


def summary_kernel(phi, y, rates, loads, message, total, spread):
    step = pl.program_id(0)

    @pl.when(step == 0)
    def _():
        total[...] = jnp.zeros_like(total)

    total[...] += contract_rows(y[...], phi[...])

    @pl.when(step == pl.num_programs(0) - 1)
    def _():
        store_by_trait(total[...], spread, message)
        groups = total.shape[1] // LANES
        pieces = []
        for vector in (rates, loads):
            width = vector.shape[1] // LANES
            parts = [split(vector[:, h * LANES : (h + 1) * LANES]) for h in range(width)]
            pieces += [part[0] for part in parts] + [part[1] for part in parts]
        tail = jnp.concatenate([piece.astype(F32) for piece in pieces], axis=0).astype(BF16)
        message[:, groups : groups + tail.shape[0], :] = jnp.broadcast_to(
            tail[None], (message.shape[0],) + tail.shape
        )


def forward_kernel(
    count, message, mixing, pattern, reply, previous, rates, loads, wide, tiles
):
    devices, rows, _ = message.shape
    owners = devices // count
    groups = mixing.shape[0] // LANES
    halves = groups // owners
    wide[...] = message[...].astype(F32).reshape(devices * rows, LANES)
    step = owners * rows

    def column(row):
        return wide[pl.ds(row, count, stride=step), :]

    summary = []
    for s in range(groups):
        block = column(s)
        for b in range(1, owners):
            block = block + column(b * rows + s)
        summary.append(block.astype(BF16))
    summary = jnp.concatenate(summary, axis=1)
    for b in range(owners):
        for h in range(halves):
            at = b * rows + groups + h
            rates_block = column(at) + column(at + halves)
            tiles[pl.ds(b * halves + h, count, stride=groups), :] = rates_block
    rates[...] = tiles[...].reshape(count, groups, LANES)
    load_rows = []
    for b in range(owners):
        for h in range(halves):
            at = b * rows + groups + 2 * halves + h
            load_rows.append(wide[at : at + 1, :] + wide[at + halves : at + halves + 1, :])
    loads[...] = jnp.concatenate(load_rows, axis=0)
    mask = pattern[...]
    for s in range(groups):
        kept = (summary.astype(F32) * mask[s : s + 1, :]).astype(BF16)
        product = contract_lanes(kept, mixing[s * LANES : (s + 1) * LANES, :])
        tiles[pl.ds(s, count, stride=groups), :] = product + summary[
            :, s * LANES : (s + 1) * LANES
        ].astype(F32)
    carried = jnp.zeros((groups, LANES), F32)
    scale = loads[...]
    for r in range(count):
        previous[r] = carried
        carried = rates[r] * carried + tiles[r * groups : (r + 1) * groups, :]
        value = (scale * carried).astype(BF16)
        for b in range(owners):
            reply[r * owners + b] = value


def residual_kernel(phi, y, arrived, message, weights, total, spread):
    step = pl.program_id(0)

    @pl.when(step == 0)
    def _():
        total[...] = jnp.zeros_like(total)
        load_by_trait(arrived, spread, weights, 0)

    fitted = contract_lanes(phi[...], weights[...])
    residual = (fitted - y[...].astype(F32)).astype(BF16)
    total[...] += contract_rows(residual, phi[...])

    @pl.when(step == pl.num_programs(0) - 1)
    def _():
        store_by_trait(total[...], spread, message)


def backward_kernel(
    count, traits, message, mixing, pattern, previous, rates, loads, reply, tiles
):
    devices = message.shape[0]
    owners = devices // count
    groups = mixing.shape[0] // LANES
    halves = groups // owners
    scale = loads[...]
    adjoint = jnp.zeros((groups, LANES), F32)
    for r in reversed(range(count)):
        pulled = message[r * owners].astype(F32)
        for b in range(1, owners):
            pulled = pulled + message[r * owners + b].astype(F32)
        pulled = scale * pulled
        if r + 1 < count:
            adjoint = pulled + rates[r + 1] * adjoint
        else:
            adjoint = pulled
        tiles[r * groups : (r + 1) * groups, :] = adjoint
        slope = adjoint * previous[r] * (1.0 / traits)
        high, low = split(slope)
        high, low = high.astype(F32), low.astype(F32)
        for b in range(owners):
            mine = slice(b * halves, (b + 1) * halves)
            tail = jnp.concatenate(
                [high[mine], low[mine], jnp.zeros((groups - 2 * halves, LANES), F32)], axis=0
            )
            reply[r * owners + b, groups : 2 * groups, :] = tail.astype(BF16)
    blocks = [tiles[pl.ds(s, count, stride=groups), :].astype(BF16) for s in range(groups)]
    adjoints = jnp.concatenate(blocks, axis=1)
    mask = pattern[...]
    for s in range(groups):
        kept = (adjoints.astype(F32) * mask[s : s + 1, :]).astype(BF16)
        product = jnp.dot(
            kept, mixing[:, s * LANES : (s + 1) * LANES], preferred_element_type=F32
        )
        tiles[pl.ds(s, count, stride=groups), :] = product + blocks[s].astype(F32)
    for r in range(count):
        back = tiles[r * groups : (r + 1) * groups, :].astype(BF16)
        for b in range(owners):
            reply[r * owners + b, 0:groups, :] = back


def gradient_kernel(halves, phi, y, loaded, arrived, out, slope, weights, spread):
    traits = loaded.shape[0]
    groups = weights.shape[1] // LANES

    @pl.when(pl.program_id(0) == 0)
    def _():
        load_by_trait(arrived, spread, weights, 0)
        load_by_trait(loaded, spread, weights, traits)
        tail = jnp.sum(arrived[:, groups : 2 * groups, :].astype(F32), axis=0)
        for h in range(halves):
            slope[:, h * LANES : (h + 1) * LANES] = (
                tail[h : h + 1, :] + tail[halves + h : halves + h + 1, :]
            )

    both = contract_lanes(phi[...], weights[...])
    residual = (both[:, traits:] - y[...].astype(F32)).astype(BF16)
    out[...] = (both[:, :traits] - residual.astype(F32)).astype(BF16)


def shards(count, observations, basis_values, mixing, pattern, decays, loadings):
    devices = lax.axis_size("region") * lax.axis_size("basis")
    rows, width = basis_values.shape
    traits = observations.shape[1]
    groups = width // LANES
    share = decays.shape[1]
    halves = share // LANES
    tile = min(TILE_ROWS, rows)
    grid = (rows // tile,)
    mixing_all = lax.all_gather(mixing, "basis", axis=0, tiled=True)
    expanded = jnp.repeat(pattern.astype(F32), BLOCK, axis=1)
    expanded_t = jnp.repeat(pattern.T.astype(F32), BLOCK, axis=1)

    def block(shape):
        return pl.BlockSpec(shape, lambda i: (0,) * len(shape))

    phi_spec = pl.BlockSpec((tile, width), lambda i: (i, 0))
    y_spec = pl.BlockSpec((tile, traits), lambda i: (i, 0))
    total = pltpu.VMEM((traits, width), F32)
    spread = pltpu.VMEM((traits * groups, LANES), F32)
    tiles = pltpu.VMEM((count * groups, LANES), F32)

    def exchange(value):
        return lax.all_to_all(value, ALL, 0, 0, tiled=True)

    sums = pl.pallas_call(
        summary_kernel,
        grid=grid,
        in_specs=[phi_spec, y_spec, block((1, share)), block((1, share))],
        out_specs=block((traits, 2 * groups, LANES)),
        out_shape=jax.ShapeDtypeStruct((traits, 2 * groups, LANES), BF16),
        scratch_shapes=[total, spread],
        compiler_params=compiler_params(),
        name="summary",
    )(basis_values, observations, decays, loadings[None, :])
    sums = exchange(sums)
    loaded, previous, rates, loads = pl.pallas_call(
        functools.partial(forward_kernel, count),
        out_shape=(
            jax.ShapeDtypeStruct((devices, groups, LANES), BF16),
            jax.ShapeDtypeStruct((count, groups, LANES), F32),
            jax.ShapeDtypeStruct((count, groups, LANES), F32),
            jax.ShapeDtypeStruct((groups, LANES), F32),
        ),
        scratch_shapes=[pltpu.VMEM((devices * 2 * groups, LANES), F32), tiles],
        compiler_params=pltpu.CompilerParams(vmem_limit_bytes=VMEM_LIMIT),
        name="forward",
    )(sums, mixing_all, expanded)
    loaded = exchange(loaded)
    pulled = pl.pallas_call(
        residual_kernel,
        grid=grid,
        in_specs=[phi_spec, y_spec, block((traits, groups, LANES))],
        out_specs=block((traits, groups, LANES)),
        out_shape=jax.ShapeDtypeStruct((traits, groups, LANES), BF16),
        scratch_shapes=[pltpu.VMEM((traits, width), BF16), total, spread],
        compiler_params=compiler_params(),
        name="residual",
    )(basis_values, observations, loaded)
    pulled = exchange(pulled)
    back = pl.pallas_call(
        functools.partial(backward_kernel, count, traits),
        out_shape=jax.ShapeDtypeStruct((devices, 2 * groups, LANES), BF16),
        scratch_shapes=[tiles],
        compiler_params=pltpu.CompilerParams(vmem_limit_bytes=VMEM_LIMIT),
        name="backward",
    )(pulled, mixing_all, expanded_t, previous, rates, loads)
    back = exchange(back)
    obs_grad, slope = pl.pallas_call(
        functools.partial(gradient_kernel, halves),
        grid=grid,
        in_specs=[
            phi_spec,
            y_spec,
            block((traits, groups, LANES)),
            block((traits, 2 * groups, LANES)),
        ],
        out_specs=(y_spec, block((1, share))),
        out_shape=(
            jax.ShapeDtypeStruct((rows, traits), BF16),
            jax.ShapeDtypeStruct((1, share), F32),
        ),
        scratch_shapes=[pltpu.VMEM((2 * traits, width), BF16), spread],
        compiler_params=compiler_params(),
        name="gradient",
    )(basis_values, observations, loaded, back)
    return obs_grad, slope


def solution(mesh):
    in_specs = (
        P(ALL, None),
        P(ALL, None),
        P("basis", None),
        P(),
        P("region", "basis"),
        P("basis"),
    )
    out_specs = (P(ALL, None), P("region", "basis"))
    body = functools.partial(shards, mesh.shape["region"])
    return jax.shard_map(body, mesh=mesh, in_specs=in_specs, out_specs=out_specs, check_vma=False)
```

time: 339 us -> 146 us (0.43); the launches traced: 334 us -> 145 us
  waiting for transfers between devices: 128 us -> 30 us
  other arithmetic: 68.1 us -> 0.01 us
  matrix products: 51.1 us -> 0 us
  Pallas kernels: 0 us -> 45.3 us
  blocking collectives: 59.2 us -> 38.6 us
  starting transfers between devices: 0.21 us -> 15.4 us
  local copies, waits for them, and re-layouts: 12.3 us -> 2.12 us
    select_n x64 -> x0, other arithmetic: 63.8 us -> none  [the longest x62 63.8 us: turn(): jnp.where(position < mine, new, old)]
    all_gather x2 -> x1, waiting for transfers between devices: 68.8 us -> 5.29 us  [shards(): mixing_all = lax.all_gather(mixing, 'basis', axis=0, tiled=True)]
    all_gather x4 -> x0, blocking collectives: 59.2 us -> none  [the longest x1 29.1 us: entering(): pieces = jax.tree.map(lambda part: lax.all_gather(part, axis), value)]
    reduce_scatter x3 -> x0, waiting for transfers between devices: 58.7 us -> none  [the longest x1 21.3 us: shards(): lax.psum_scatter(contract_rows(basis_values, observations), 'basis', scat...]
    dot_general x7 -> x0, matrix products: 51.1 us -> none  [the longest x2 24.8 us: predict_piece(): return jnp.dot(basis_values, piece, preferred_element_type=jnp.float32)]
    pallas_call x0 -> x5, Pallas kernels: none -> 45.3 us  [the longest x1 15.4 us: shards(): pl.pallas_call(residual_kernel, grid=grid, in_specs=[phi_spec, y_spec, bl...]
    all_to_all x0 -> x2, blocking collectives: none -> 38.6 us  [exchange(): return lax.all_to_all(value, ALL, 0, 0, tiled=True)]
    all_to_all x0 -> x2, waiting for transfers between devices: none -> 24 us  [exchange(): return lax.all_to_all(value, ALL, 0, 0, tiled=True)]
  transfers between devices with their start and end apart: 5 -> 3, of which waited for: 5 -> 3; matrix products, arithmetic and copies ran while one was open for 2% -> 1% of each run, Pallas kernels for 0% -> 7%
where the time goes in v1:
time: 146 us; the launch traced here: 145 us
  Pallas kernels  45.3 us (31%)
  blocking collectives  38.6 us (26%)
  waiting for transfers between devices  30 us (21%)
  starting transfers between devices  15.4 us (11%)
  between operations  14.1 us (10%)
  local copies, waits for them, and re-layouts  2.12 us (1%)
    all_to_all x2, blocking collectives, exchange(): return lax.all_to_all(value, ALL, 0, 0, tiled=True)  38.6 us
    all_to_all x2, waiting for transfers between devices, exchange(): return lax.all_to_all(value, ALL, 0, 0, tiled=True)  24 us
    all_to_all x2, starting transfers between devices, exchange(): return lax.all_to_all(value, ALL, 0, 0, tiled=True)  15.4 us
    pallas_call x1, Pallas kernels, shards(): pl.pallas_call(residual_kernel, grid=grid, in_specs=[phi_spec, y_spec, bl...  15.4 us
    pallas_call x1, Pallas kernels, shards(): pl.pallas_call(functools.partial(gradient_kernel, halves), grid=grid, in_...  12.4 us
    pallas_call x1, Pallas kernels, shards(): pl.pallas_call(summary_kernel, grid=grid, in_specs=[phi_spec, y_spec, blo...  10.5 us
    all_gather x1, waiting for transfers between devices, shards(): mixing_all = lax.all_gather(mixing, 'basis', axis=0, tiled=True)  5.29 us
    pallas_call x1, Pallas kernels, shards(): pl.pallas_call(functools.partial(forward_kernel, count), out_shape=(jax.S...  3.63 us
  transfers between devices with their start and end apart: 3, of which 3 were waited for; matrix products, arithmetic and copies ran while one was open for 1% of the time, Pallas kernels for 7%

profile of v1, /device:TPU:1, one launch (start us, length us, event | category | flops | bytes accessed | tf_op | source)
XLA Modules:
  0.0 145.5 jit_solution(12127978580814901459)
XLA Ops:
  7.2 0.0 all-gather.2.cloned.1.call-start
  7.2 0.7 all-gather.2.cloned.1.call-update
  7.9 0.0 copy-start.2
  7.9 10.5 %summary.1 = bf16[128,16,128]{2,1,0:T(8,128)(2,1)} custom-call(bf16[8192,1024]{1,0:T(8,128)(2,1)} %phi.5, bf16[8192,128]{1,0:T(8,128)(2,1)} %y.5, f32[1,256]{1,0:T(1,128)} %rates.1, f32[1,256]{1,0:T(1,128)} %bitcast.7), custom_call_target="tpu_custom_call" | custom-call | tf_op jit(solution)/shard_map/summary/pallas_call | solution.py:233
  18.4 11.5 %all-to-all-start = ((bf16[128,16,128]{2,1,0:T(8,128)(2,1)}), bf16[128,16,128]{2,1,0:T(8,128)(2,1)S(1)}, u32[]{:S(2)}, u32[]{:S(2)}) async-start(bf16[128,16,128]{2,1,0:T(8,128)(2,1)} %summary.1), calls=%async_computation | async-start | bytes 1048576 | tf_op jit(solution)/shard_map/all_to_all | solution.py:231
  29.9 0.0 copy-done.2
  30.0 0.1 copy.8
  30.0 0.7 broadcast_bitcast_fusion.1.pattern
  30.7 13.4 %all-to-all-done.message = bf16[128,16,128]{2,1,0:T(8,128)(2,1)S(1)} async-done(((bf16[128,16,128]{2,1,0:T(8,128)(2,1)}), bf16[128,16,128]{2,1,0:T(8,128)(2,1)S(1)}, u32[]{:S(2)}, u32[]{:S(2)}) %all-to-all-start) | async-done | bytes 524320 | tf_op jit(solution)/shard_map/all_to_all | solution.py:231
  44.1 0.0 copy-start
  44.1 5.3 %all-gather.2.cloned.1.call-done.mixing = bf16[1024,1024]{1,0:T(8,128)(2,1)} async-done(((bf16[256,1024]{1,0:T(8,128)(2,1)}), bf16[1024,1024]{1,0:T(8,128)(2,1)}) %all-gather.2.cloned.1.call-update) | async-done | bytes 2097168 | tf_op jit(solution)/shard_map/all_gather | solution.py:217
  49.4 0.0 copy-done
  49.4 3.6 %forward.1 = (bf16[128,8,128]{2,1,0:T(8,128)(2,1)}, f32[32,8,128]{2,1,0:T(8,128)}, f32[32,8,128]{2,1,0:T(8,128)}, f32[8,128]{1,0:T(8,128)}) custom-call(bf16[128,16,128]{2,1,0:T(8,128)(2,1)} %copy-done, bf16[1024,1024]{1,0:T(8,128)(2,1)} %all-gather.2.cloned.1.call-done.mixing, f32[8,1024]{1,0:T(8,128)} %broadcast_bitcast_fusion.1.pattern), custom_call_target="tpu_custom_call" | custom-call | tf_op jit(solution)/shard_map/forward/pallas_call | solution.py:244
  53.0 19.7 %all_to_all.20.arrived.loaded = bf16[128,8,128]{2,1,0:T(8,128)(2,1)} all-to-all(bf16[128,8,128]{2,1,0:T(8,128)(2,1)} %get-tuple-element.6), channel_id=1, replica_groups=mesh['region'=32,'basis'=4] {'region','basis'}, dimensions={0} | all-to-all | bytes 524288 | tf_op jit(solution)/shard_map/all_to_all | solution.py:231
  72.7 15.4 %residual.1 = bf16[128,8,128]{2,1,0:T(8,128)(2,1)} custom-call(bf16[8192,1024]{1,0:T(8,128)(2,1)} %phi.5, bf16[8192,128]{1,0:T(8,128)(2,1)} %y.5, bf16[128,8,128]{2,1,0:T(8,128)(2,1)} %all_to_all.20.arrived.loaded), custom_call_target="tpu_custom_call" | custom-call | tf_op jit(solution)/shard_map/residual/pallas_call | solution.py:257
  88.1 3.9 %all-to-all-start.2 = ((bf16[128,8,128]{2,1,0:T(8,128)(2,1)}), bf16[128,8,128]{2,1,0:T(8,128)(2,1)S(1)}, u32[]{:S(2)}, u32[]{:S(2)}) async-start(bf16[128,8,128]{2,1,0:T(8,128)(2,1)} %residual.1), calls=%async_computation.2 | async-start | bytes 524288 | tf_op jit(solution)/shard_map/all_to_all | solution.py:231
  92.0 0.7 broadcast_bitcast_fusion.pattern
  92.7 10.7 %all-to-all-done.2.message = bf16[128,8,128]{2,1,0:T(8,128)(2,1)S(1)} async-done(((bf16[128,8,128]{2,1,0:T(8,128)(2,1)}), bf16[128,8,128]{2,1,0:T(8,128)(2,1)S(1)}, u32[]{:S(2)}, u32[]{:S(2)}) %all-to-all-start.2) | async-done | bytes 262176 | tf_op jit(solution)/shard_map/all_to_all | solution.py:231
  103.3 0.0 copy-start.1
  103.3 0.7 copy-done.1
  104.0 3.4 %backward.1 = bf16[128,16,128]{2,1,0:T(8,128)(2,1)} custom-call(bf16[128,8,128]{2,1,0:T(8,128)(2,1)} %copy-done.1, bf16[1024,1024]{1,0:T(8,128)(2,1)} %all-gather.2.cloned.1.call-done.mixing, f32[8,1024]{1,0:T(8,128)} %broadcast_bitcast_fusion.pattern, f32[32,8,128]{2,1,0:T(8,128)} %get-tuple-element.7.previous, f32[32,8,128]{2,1,0:T(8,128)} %get-tuple-element.8.rates, ...), custom_call_target="tpu_custom_call" | custom-call | tf_op jit(solution)/shard_map/backward/pallas_call | solution.py:268
  107.4 18.9 %all_to_all.21.arrived = bf16[128,16,128]{2,1,0:T(8,128)(2,1)} all-to-all(bf16[128,16,128]{2,1,0:T(8,128)(2,1)} %backward.1), channel_id=1, replica_groups=mesh['region'=32,'basis'=4] {'region','basis'}, dimensions={0} | all-to-all | bytes 1048576 | tf_op jit(solution)/shard_map/all_to_all | solution.py:231
  126.2 12.4 %gradient.1 = (bf16[8192,128]{1,0:T(8,128)(2,1)}, f32[1,256]{1,0:T(1,128)}) custom-call(bf16[8192,1024]{1,0:T(8,128)(2,1)} %phi.5, bf16[8192,128]{1,0:T(8,128)(2,1)} %y.5, bf16[128,8,128]{2,1,0:T(8,128)(2,1)} %all_to_all.20.arrived.loaded, bf16[128,16,128]{2,1,0:T(8,128)(2,1)} %all_to_all.21.arrived), custom_call_target="tpu_custom_call" | custom-call | tf_op jit(solution)/shard_map/gradient/pallas_call | solution.py:276
  (1 shorter events, 0.0 us)
Async XLA Ops:
  7.2 42.2 %all-gather.2.cloned.1.call-start = ((), (), s32[]{:S(2)}) async-start(), calls=%async_computation.4 | async-start | bytes 2621440 | tf_op jit(solution)/shard_map/all_gather | solution.py:217
  7.9 22.1 %copy-start.2 = (s32[8,8]{1,0:T(8,128)S(1)}, s32[8,8]{1,0:T(8,128)}, u32[]{:S(2)}) copy-start(s32[8,8]{1,0:T(8,128)} %param.9) | copy-start | bytes 772
  18.4 25.7 %all-to-all-start = ((bf16[128,16,128]{2,1,0:T(8,128)(2,1)}), bf16[128,16,128]{2,1,0:T(8,128)(2,1)S(1)}, u32[]{:S(2)}, u32[]{:S(2)}) async-start(bf16[128,16,128]{2,1,0:T(8,128)(2,1)} %summary.1), calls=%async_computation | async-start | bytes 1048576 | tf_op jit(solution)/shard_map/all_to_all | solution.py:231
  44.1 5.3 %copy-start = (bf16[128,16,128]{2,1,0:T(8,128)(2,1)}, bf16[128,16,128]{2,1,0:T(8,128)(2,1)S(1)}, u32[]{:S(2)}) copy-start(bf16[128,16,128]{2,1,0:T(8,128)(2,1)S(1)} %all-to-all-done.message) | copy-start | bytes 1572868
  88.1 15.2 %all-to-all-start.2 = ((bf16[128,8,128]{2,1,0:T(8,128)(2,1)}), bf16[128,8,128]{2,1,0:T(8,128)(2,1)S(1)}, u32[]{:S(2)}, u32[]{:S(2)}) async-start(bf16[128,8,128]{2,1,0:T(8,128)(2,1)} %residual.1), calls=%async_computation.2 | async-start | bytes 524288 | tf_op jit(solution)/shard_map/all_to_all | solution.py:231
  103.3 0.7 copy-start.1
Sparse Core Ops, SparseCore 0:
  9.7 39.6 all-gather.1

commit v2 on v1

v2 whole, which is shorter than its diff:
```python
import functools

import jax
import jax.numpy as jnp
from jax import lax
from jax.experimental import pallas as pl
from jax.experimental.pallas import tpu as pltpu
from jax.sharding import PartitionSpec as P

BLOCK = 128
LANES = 128
TILE_ROWS = 1024
VMEM_LIMIT = 48 * 1024 * 1024
ALL = ("region", "basis")
F32 = jnp.float32
BF16 = jnp.bfloat16
OWNERS = 4


def split(value):
    high = value.astype(BF16)
    return high, (value - high.astype(F32)).astype(BF16)


def start_chunks(tile, pairs, sems):
    rows = pairs[0][0].shape[0]
    chunks = []
    for i in range(rows // tile):
        at = pl.ds(i * tile, tile)
        copies = [
            pltpu.make_async_copy(source.at[at], target.at[at], sems.at[k, i])
            for k, (source, target) in enumerate(pairs)
        ]
        for copy in copies:
            copy.start()
        chunks.append((at, copies))
    return chunks


def wait_all(copies):
    for copy in copies:
        copy.wait()


def start_mixing(pieces, mixing, sems):
    own, near, far, near_other, far_other = pieces
    share, part = own.shape[0], far.shape[0]
    owner = lax.axis_index("basis")
    core = lax.rem(lax.axis_index("region"), 2)
    across = lax.rem(owner + 2, OWNERS) * share
    starts = (
        owner * share,
        lax.rem(owner + 3 + 2 * core, OWNERS) * share,
        across + core * part,
        lax.rem(owner + 1 + 2 * core, OWNERS) * share,
        across + (1 - core) * part,
    )
    copies = []
    for k, (piece, start) in enumerate(zip(pieces, starts)):
        at = pl.ds(pl.multiple_of(start, part), piece.shape[0])
        copies.append(pltpu.make_async_copy(piece, mixing.at[at], sems.at[k]))
        copies[-1].start()
    return copies


def keep(blocks, present):
    return jnp.concatenate(
        [(block * flag.astype(F32)).astype(BF16) for block, flag in zip(blocks, present)], axis=1
    )


def contract_lanes(first, second):
    return lax.dot_general(first, second, (((1,), (1,)), ((), ())), preferred_element_type=F32)


def store_by_trait(total, spread, message):
    traits, width = total.shape
    groups = width // LANES
    for s in range(groups):
        spread[pl.ds(s, traits, stride=groups), :] = total[:, s * LANES : (s + 1) * LANES]
    message[:, 0:groups, :] = spread[...].reshape(traits, groups, LANES).astype(BF16)


def load_by_trait(message, spread, target, at):
    traits = message.shape[0]
    groups = target.shape[1] // LANES
    spread[...] = message[:, 0:groups, :].astype(F32).reshape(traits * groups, LANES)
    for s in range(groups):
        target[at : at + traits, s * LANES : (s + 1) * LANES] = spread[
            pl.ds(s, traits, stride=groups), :
        ].astype(BF16)


def summary_kernel(tile, phi, y, rates, loads, message, phi_here, y_here, total, spread, sems):
    chunks = start_chunks(tile, ((y, y_here), (phi, phi_here)), sems)
    for i, (at, copies) in enumerate(chunks):
        wait_all(copies)
        product = jnp.dot(y_here[at, :].T, phi_here[at, :], preferred_element_type=F32)
        if i == 0:
            total[...] = product
        else:
            total[...] += product
    store_by_trait(total[...], spread, message)
    groups = total.shape[1] // LANES
    pieces = []
    for vector in (rates, loads):
        width = vector.shape[1] // LANES
        parts = [split(vector[:, h * LANES : (h + 1) * LANES]) for h in range(width)]
        pieces += [part[0] for part in parts] + [part[1] for part in parts]
    tail = jnp.concatenate([piece.astype(F32) for piece in pieces], axis=0).astype(BF16)
    message[:, groups : groups + tail.shape[0], :] = jnp.broadcast_to(
        tail[None], (message.shape[0],) + tail.shape
    )


def forward_kernel(count, message, pattern, *refs):
    *pieces, reply, previous, rates, loads, mixing, wide, tiles, sems = refs
    copies = start_mixing(pieces, mixing, sems)
    devices, rows, _ = message.shape
    owners = devices // count
    groups = mixing.shape[0] // LANES
    halves = groups // owners
    wide[...] = message[...].astype(F32).reshape(devices * rows, LANES)
    step = owners * rows

    def column(row):
        return wide[pl.ds(row, count, stride=step), :]

    summary = []
    for s in range(groups):
        block = column(s)
        for b in range(1, owners):
            block = block + column(b * rows + s)
        summary.append(block.astype(BF16).astype(F32))
    for b in range(owners):
        for h in range(halves):
            at = b * rows + groups + h
            rates_block = column(at) + column(at + halves)
            tiles[pl.ds(b * halves + h, count, stride=groups), :] = rates_block
    rates[...] = tiles[...].reshape(count, groups, LANES)
    load_rows = []
    for b in range(owners):
        for h in range(halves):
            at = b * rows + groups + 2 * halves + h
            load_rows.append(wide[at : at + 1, :] + wide[at + halves : at + halves + 1, :])
    loads[...] = jnp.concatenate(load_rows, axis=0)
    wait_all(copies)
    for s in range(groups):
        kept = keep(summary, [pattern[s, k] for k in range(groups)])
        product = contract_lanes(kept, mixing[s * LANES : (s + 1) * LANES, :])
        tiles[pl.ds(s, count, stride=groups), :] = product + summary[s]
    carried = jnp.zeros((groups, LANES), F32)
    scale = loads[...]
    for r in range(count):
        previous[r] = carried
        carried = rates[r] * carried + tiles[r * groups : (r + 1) * groups, :]
        value = (scale * carried).astype(BF16)
        for b in range(owners):
            reply[r * owners + b] = value


def residual_kernel(
    tile, phi, y, arrived, message, phi_here, y_here, weights, total, spread, sems
):
    chunks = start_chunks(tile, ((y, y_here), (phi, phi_here)), sems)
    load_by_trait(arrived, spread, weights, 0)
    for i, (at, copies) in enumerate(chunks):
        wait_all(copies)
        fitted = contract_lanes(weights[...], phi_here[at, :])
        residual = (fitted - y_here[at, :].T.astype(F32)).astype(BF16)
        product = jnp.dot(residual, phi_here[at, :], preferred_element_type=F32)
        if i == 0:
            total[...] = product
        else:
            total[...] += product
    store_by_trait(total[...], spread, message)


def backward_kernel(count, traits, message, pattern, previous, rates, loads, *refs):
    *pieces, reply, mixing, tiles, sems = refs
    copies = start_mixing(pieces, mixing, sems)
    devices = message.shape[0]
    owners = devices // count
    groups = mixing.shape[0] // LANES
    halves = groups // owners
    scale = loads[...]
    adjoint = jnp.zeros((groups, LANES), F32)
    for r in reversed(range(count)):
        pulled = message[r * owners].astype(F32)
        for b in range(1, owners):
            pulled = pulled + message[r * owners + b].astype(F32)
        pulled = scale * pulled
        if r + 1 < count:
            adjoint = pulled + rates[r + 1] * adjoint
        else:
            adjoint = pulled
        tiles[r * groups : (r + 1) * groups, :] = adjoint
        slope = adjoint * previous[r] * (1.0 / traits)
        high, low = split(slope)
        high, low = high.astype(F32), low.astype(F32)
        for b in range(owners):
            mine = slice(b * halves, (b + 1) * halves)
            tail = jnp.concatenate(
                [high[mine], low[mine], jnp.zeros((groups - 2 * halves, LANES), F32)], axis=0
            )
            reply[r * owners + b, groups : 2 * groups, :] = tail.astype(BF16)
    blocks = [
        tiles[pl.ds(s, count, stride=groups), :].astype(BF16).astype(F32) for s in range(groups)
    ]
    wait_all(copies)
    for s in range(groups):
        kept = keep(blocks, [pattern[k, s] for k in range(groups)])
        product = jnp.dot(
            kept, mixing[:, s * LANES : (s + 1) * LANES], preferred_element_type=F32
        )
        tiles[pl.ds(s, count, stride=groups), :] = product + blocks[s]
    for r in range(count):
        back = tiles[r * groups : (r + 1) * groups, :].astype(BF16)
        for b in range(owners):
            reply[r * owners + b, 0:groups, :] = back


def gradient_kernel(
    tile,
    halves,
    phi,
    y,
    loaded,
    arrived,
    out,
    slope,
    phi_here,
    y_here,
    out_here,
    weights,
    spread,
    sems,
):
    chunks = start_chunks(tile, ((y, y_here), (phi, phi_here)), sems)
    traits = loaded.shape[0]
    groups = weights.shape[1] // LANES
    load_by_trait(arrived, spread, weights, 0)
    load_by_trait(loaded, spread, weights, traits)
    tail = jnp.sum(arrived[:, groups : 2 * groups, :].astype(F32), axis=0)
    for h in range(halves):
        slope[:, h * LANES : (h + 1) * LANES] = (
            tail[h : h + 1, :] + tail[halves + h : halves + h + 1, :]
        )
    stores = []
    for i, (at, copies) in enumerate(chunks):
        wait_all(copies)
        both = contract_lanes(weights[...], phi_here[at, :])
        residual = (both[traits:] - y_here[at, :].T.astype(F32)).astype(BF16)
        out_here[at, :] = (both[:traits] - residual.astype(F32)).astype(BF16).T
        stores.append(pltpu.make_async_copy(out_here.at[at], out.at[at], sems.at[2, i]))
        stores[-1].start()
    wait_all(stores)


def mixing_pieces(mixing):
    regions = lax.axis_size("region")
    part = mixing.shape[0] // 2
    core = lax.rem(lax.axis_index("region"), 2)
    half = lax.dynamic_slice_in_dim(mixing, core * part, part, 0)

    def move(value, target):
        pairs = [
            (r * OWNERS + b, target(r, b)) for r in range(regions) for b in range(OWNERS)
        ]
        return lax.ppermute(value, ALL, pairs)

    def beside(r, b):
        return r * OWNERS + (b + 1 + 2 * (r % 2)) % OWNERS

    def across(r, b):
        return r * OWNERS + (b + 2) % OWNERS

    def other_core(r, b):
        return (r ^ 1) * OWNERS + b

    def swap(near, far):
        return mixing, near, far, move(near, other_core), move(far, other_core)

    return (move(mixing, beside), move(half, across)), swap


def shards(count, observations, basis_values, mixing, pattern, decays, loadings):
    devices = lax.axis_size("region") * lax.axis_size("basis")
    rows, width = basis_values.shape
    traits = observations.shape[1]
    groups = width // LANES
    share = decays.shape[1]
    halves = share // LANES
    tile = min(TILE_ROWS, rows)
    chunks = rows // tile
    fetched, swap = mixing_pieces(mixing)

    hbm = pl.BlockSpec(memory_space=pl.ANY)
    vmem = pl.BlockSpec(memory_space=pltpu.VMEM)
    smem = pl.BlockSpec(memory_space=pltpu.SMEM)
    params = pltpu.CompilerParams(vmem_limit_bytes=VMEM_LIMIT)
    phi_here = pltpu.VMEM((rows, width), BF16)
    y_here = pltpu.VMEM((rows, traits), BF16)
    total = pltpu.VMEM((traits, width), F32)
    spread = pltpu.VMEM((traits * groups, LANES), F32)
    tiles = pltpu.VMEM((count * groups, LANES), F32)
    mixing_here = pltpu.VMEM((width, width), BF16)
    short = jax.ShapeDtypeStruct((devices, groups, LANES), BF16)
    long = jax.ShapeDtypeStruct((devices, 2 * groups, LANES), BF16)

    def sems(*shape):
        return pltpu.SemaphoreType.DMA(shape)

    def exchange(value):
        return lax.all_to_all(value, ALL, 0, 0, tiled=True)

    sums = pl.pallas_call(
        functools.partial(summary_kernel, tile),
        in_specs=[hbm, hbm, vmem, vmem],
        out_specs=vmem,
        out_shape=long,
        scratch_shapes=[phi_here, y_here, total, spread, sems(2, chunks)],
        compiler_params=params,
        name="summary",
    )(basis_values, observations, decays, loadings[None, :])
    sums, fetched = lax.optimization_barrier((sums, fetched))
    pieces = swap(*fetched)
    sums = exchange(sums)
    loaded, previous, rates, loads = pl.pallas_call(
        functools.partial(forward_kernel, count),
        in_specs=[vmem, smem] + [hbm] * len(pieces),
        out_specs=(vmem,) * 4,
        out_shape=(
            short,
            jax.ShapeDtypeStruct((count, groups, LANES), F32),
            jax.ShapeDtypeStruct((count, groups, LANES), F32),
            jax.ShapeDtypeStruct((groups, LANES), F32),
        ),
        scratch_shapes=[
            mixing_here,
            pltpu.VMEM((devices * 2 * groups, LANES), F32),
            tiles,
            sems(len(pieces)),
        ],
        compiler_params=params,
        name="forward",
    )(sums, pattern, *pieces)
    loaded = exchange(loaded)
    pulled = pl.pallas_call(
        functools.partial(residual_kernel, tile),
        in_specs=[hbm, hbm, vmem],
        out_specs=vmem,
        out_shape=short,
        scratch_shapes=[
            phi_here,
            y_here,
            pltpu.VMEM((traits, width), BF16),
            total,
            spread,
            sems(2, chunks),
        ],
        compiler_params=params,
        name="residual",
    )(basis_values, observations, loaded)
    pulled = exchange(pulled)
    back = pl.pallas_call(
        functools.partial(backward_kernel, count, traits),
        in_specs=[vmem, smem, vmem, vmem, vmem] + [hbm] * len(pieces),
        out_specs=vmem,
        out_shape=long,
        scratch_shapes=[mixing_here, tiles, sems(len(pieces))],
        compiler_params=params,
        name="backward",
    )(pulled, pattern, previous, rates, loads, *pieces)
    back = exchange(back)
    obs_grad, slope = pl.pallas_call(
        functools.partial(gradient_kernel, tile, halves),
        in_specs=[hbm, hbm, vmem, vmem],
        out_specs=(hbm, vmem),
        out_shape=(
            jax.ShapeDtypeStruct((rows, traits), BF16),
            jax.ShapeDtypeStruct((1, share), F32),
        ),
        scratch_shapes=[
            phi_here,
            y_here,
            y_here,
            pltpu.VMEM((2 * traits, width), BF16),
            spread,
            sems(3, chunks),
        ],
        compiler_params=params,
        name="gradient",
    )(basis_values, observations, loaded, back)
    return obs_grad, slope


def solution(mesh):
    in_specs = (
        P(ALL, None),
        P(ALL, None),
        P("basis", None),
        P(),
        P("region", "basis"),
        P("basis"),
    )
    out_specs = (P(ALL, None), P("region", "basis"))
    body = functools.partial(shards, mesh.shape["region"])
    return jax.shard_map(body, mesh=mesh, in_specs=in_specs, out_specs=out_specs, check_vma=False)
```

time: 146 us -> 116 us (0.79)
  waiting for transfers between devices: 30 us -> 12.5 us
  Pallas kernels: 45.3 us -> 32 us
  between operations: 14.1 us -> 0.89 us
  blocking collectives: 38.6 us -> 47.5 us
  local copies, waits for them, and re-layouts: 2.12 us -> 6.42 us
    pallas_call x5, Pallas kernels: 45.3 us -> 32 us  [the longest x1 10.2 us: shards(): pl.pallas_call(functools.partial(residual_kernel, tile), in_specs=[hbm, h...]
    all_to_all x2 -> x1, waiting for transfers between devices: 24 us -> 11.1 us  [exchange(): return lax.all_to_all(value, ALL, 0, 0, tiled=True)]
    all_to_all x2 -> x3, blocking collectives: 38.6 us -> 47.5 us  [exchange(): return lax.all_to_all(value, ALL, 0, 0, tiled=True)]
    ppermute x0 -> x4, starting transfers between devices: none -> 8.55 us  [move(): return lax.ppermute(value, ALL, pairs)]
    all_to_all x2 -> x1, starting transfers between devices: 15.4 us -> 7.76 us  [exchange(): return lax.all_to_all(value, ALL, 0, 0, tiled=True)]
    all_gather x1 -> x0, waiting for transfers between devices: 5.29 us -> none  [shards(): mixing_all = lax.all_gather(mixing, 'basis', axis=0, tiled=True)]
    unnamed x6 -> x20, local copies, waits for them, and re-layouts: 0.7 us -> 5.42 us
  transfers between devices with their start and end apart: 3 -> 5, of which waited for: 3 -> 3; matrix products, arithmetic and copies ran while one was open for 1% -> 1% of each run, Pallas kernels for 7% -> 6%
where the time goes in v2:
time: 116 us
  blocking collectives  47.5 us (41%)
  Pallas kernels  32 us (28%)
  starting transfers between devices  16.3 us (14%)
  waiting for transfers between devices  12.5 us (11%)
  local copies, waits for them, and re-layouts  6.42 us (6%)
    all_to_all x3, blocking collectives, exchange(): return lax.all_to_all(value, ALL, 0, 0, tiled=True)  47.5 us
    all_to_all x1, waiting for transfers between devices, exchange(): return lax.all_to_all(value, ALL, 0, 0, tiled=True)  11.1 us
    pallas_call x1, Pallas kernels, shards(): pl.pallas_call(functools.partial(residual_kernel, tile), in_specs=[hbm, h...  10.2 us
    pallas_call x1, Pallas kernels, shards(): pl.pallas_call(functools.partial(gradient_kernel, tile, halves), in_specs...  9.79 us
    ppermute x4, starting transfers between devices, move(): return lax.ppermute(value, ALL, pairs)  8.55 us
    all_to_all x1, starting transfers between devices, exchange(): return lax.all_to_all(value, ALL, 0, 0, tiled=True)  7.76 us
    pallas_call x1, Pallas kernels, shards(): pl.pallas_call(functools.partial(summary_kernel, tile), in_specs=[hbm, hb...  6.6 us
    unnamed x20, local copies, waits for them, and re-layouts  5.42 us
  transfers between devices with their start and end apart: 5, of which 3 were waited for; matrix products, arithmetic and copies ran while one was open for 1% of the time, Pallas kernels for 6%

profile of v2, /device:TPU:1, one launch (start us, length us, event | category | flops | bytes accessed | tf_op | source)
XLA Modules:
  0.0 115.7 jit_solution(3676161766871075371)
XLA Ops:
  0.6 3.6 %collective-permute-start = (bf16[256,1024]{1,0:T(8,128)(2,1)}, bf16[256,1024]{1,0:T(8,128)(2,1)}, u32[]{:S(2)}, u32[]{:S(2)}) collective-permute-start(bf16[256,1024]{1,0:T(8,128)(2,1)} %refs_0_.3), channel_id=1, source_target_pairs={{0,1},{1,2},{2,3},{3,0},{4,7},{5,4},{6,5},{7,6},{8,9},{9,10},{10,1... | collective-permute-start | bytes 1572872 | tf_op jit(solution)/shard_map/ppermute | solution.py:270
  4.3 1.0 constant_dynamic-slice_fusion
  5.3 0.4 collective-permute-start.1
  5.7 0.0 copy-start
  5.7 1.6 %copy-done = bf16[8192,128]{1,0:T(8,128)(2,1)S(1)} copy-done((bf16[8192,128]{1,0:T(8,128)(2,1)S(1)}, bf16[8192,128]{1,0:T(8,128)(2,1)}, u32[]{:S(2)}) %copy-start) | copy-done | bytes 2097176
  7.3 0.7 copy-done.8
  8.0 0.7 copy-done.9
  8.6 6.6 %summary.1 = bf16[128,16,128]{2,1,0:T(8,128)(2,1)S(1)} custom-call(bf16[8192,1024]{1,0:T(8,128)(2,1)} %phi.5, bf16[8192,128]{1,0:T(8,128)(2,1)S(1)} %copy-done, f32[1,256]{1,0:T(1,128)S(1)} %copy-done.8, f32[1,256]{1,0:T(1,128)S(1)} %bitcast.1), custom_call_target="tpu_custom_call" | custom-call | tf_op jit(solution)/shard_map/summary/pallas_call | solution.py:317
  15.3 0.0 copy-start.3
  15.3 0.8 copy-done.3
  16.1 0.0 collective-permute-done.1.refs_2_
  16.1 0.3 collective-permute-done.refs_1_
  16.3 3.3 %collective-permute-start.2 = (bf16[256,1024]{1,0:T(8,128)(2,1)}, bf16[256,1024]{1,0:T(8,128)(2,1)}, u32[]{:S(2)}, u32[]{:S(2)}) collective-permute-start(bf16[256,1024]{1,0:T(8,128)(2,1)} %collective-permute-done.refs_1_), channel_id=1, source_target_pairs={{0,4},{1,5},{2,6},{3,7},{4,0},{5,1},{6,2},{7,3},{8,12},{9,13},{10,... | collective-permute-start | bytes 1572872 | tf_op jit(solution)/shard_map/ppermute | solution.py:270
  19.7 7.8 %all-to-all-start = ((bf16[128,16,128]{2,1,0:T(8,128)(2,1)}), bf16[128,16,128]{2,1,0:T(8,128)(2,1)S(1)}, u32[]{:S(2)}, u32[]{:S(2)}) async-start(bf16[128,16,128]{2,1,0:T(8,128)(2,1)} %copy-done.3), calls=%async_computation | async-start | bytes 1048576 | tf_op jit(solution)/shard_map/all_to_all | solution.py:315
  27.4 1.1 collective-permute-start.3
  28.6 1.2 %collective-permute-done.3.refs_4_ = bf16[128,1024]{1,0:T(8,128)(2,1)S(1)} collective-permute-done((bf16[128,1024]{1,0:T(8,128)(2,1)S(1)}, bf16[128,1024]{1,0:T(8,128)(2,1)S(1)}, u32[]{:S(2)}, u32[]{:S(2)}) %collective-permute-start.3) | collective-permute-done | bytes 262176 | tf_op jit(solution)/shard_map/ppermute | solution.py:270
  29.7 0.7 copy-done.4
  30.5 11.1 %all-to-all-done.message = bf16[128,16,128]{2,1,0:T(8,128)(2,1)S(1)} async-done(((bf16[128,16,128]{2,1,0:T(8,128)(2,1)}), bf16[128,16,128]{2,1,0:T(8,128)(2,1)S(1)}, u32[]{:S(2)}, u32[]{:S(2)}) %all-to-all-start) | async-done | bytes 524320 | tf_op jit(solution)/shard_map/all_to_all | solution.py:315
  41.6 0.0 collective-permute-done.2.refs_3_
  41.6 0.0 copy-done.2
  41.6 0.0 copy-done.7
  41.6 0.0 copy-start.5
  41.6 0.9 copy-done.5
  42.5 2.8 %forward.1 = (bf16[128,8,128]{2,1,0:T(8,128)(2,1)S(1)}, f32[32,8,128]{2,1,0:T(8,128)S(1)}, f32[32,8,128]{2,1,0:T(8,128)S(1)}, f32[8,128]{1,0:T(8,128)S(1)}) custom-call(bf16[128,16,128]{2,1,0:T(8,128)(2,1)S(1)} %all-to-all-done.message, s32[8,8]{1,0:T(8,128)S(1)} %copy-done.7, bf16[256,1024]{1,0:T(8,128)(2,1)S(1)} %copy-done.2, ...), custom_call_target="tpu_custom_call" | custom-call | tf_op jit(solution)/shard_map/forward/pallas_call | solution.py:329
  45.3 14.7 %all_to_all.20.arrived.loaded = bf16[128,8,128]{2,1,0:T(8,128)(2,1)S(1)} all-to-all(bf16[128,8,128]{2,1,0:T(8,128)(2,1)S(1)} %get-tuple-element.12), channel_id=1, replica_groups=mesh['region'=32,'basis'=4] {'region','basis'}, dimensions={0} | all-to-all | bytes 524288 | tf_op jit(solution)/shard_map/all_to_all | solution.py:315
  60.0 0.0 copy-done.1
  60.0 10.2 %residual.1 = bf16[128,8,128]{2,1,0:T(8,128)(2,1)S(1)} custom-call(bf16[8192,1024]{1,0:T(8,128)(2,1)} %phi.5, bf16[8192,128]{1,0:T(8,128)(2,1)S(1)} %copy-done.1, bf16[128,8,128]{2,1,0:T(8,128)(2,1)S(1)} %all_to_all.20.arrived.loaded), custom_call_target="tpu_custom_call" | custom-call | tf_op jit(solution)/shard_map/residual/pallas_call | solution.py:349
  70.2 15.0 %all_to_all.21.message = bf16[128,8,128]{2,1,0:T(8,128)(2,1)S(1)} all-to-all(bf16[128,8,128]{2,1,0:T(8,128)(2,1)S(1)} %residual.1), channel_id=1, replica_groups=mesh['region'=32,'basis'=4] {'region','basis'}, dimensions={0} | all-to-all | bytes 524288 | tf_op jit(solution)/shard_map/all_to_all | solution.py:315
  85.2 0.0 copy-done.6
  85.2 2.7 %backward.1 = bf16[128,16,128]{2,1,0:T(8,128)(2,1)S(1)} custom-call(bf16[128,8,128]{2,1,0:T(8,128)(2,1)S(1)} %all_to_all.21.message, s32[8,8]{1,0:T(8,128)S(1)} %copy-done.7, f32[32,8,128]{2,1,0:T(8,128)S(1)} %get-tuple-element.13.previous, f32[32,8,128]{2,1,0:T(8,128)S(1)} %get-tuple-element.14.rates, f32[8,128]{1,0:T(8,128)S(1)} %get-tuple-element.15.loads, ...), custom_call_target="tpu_custom_call" | custom-call | tf_op jit(solution)/shard_map/backward/pallas_call | solution.py:366
  87.9 17.8 %all_to_all.22.arrived = bf16[128,16,128]{2,1,0:T(8,128)(2,1)S(1)} all-to-all(bf16[128,16,128]{2,1,0:T(8,128)(2,1)S(1)} %backward.1), channel_id=1, replica_groups=mesh['region'=32,'basis'=4] {'region','basis'}, dimensions={0} | all-to-all | bytes 1048576 | tf_op jit(solution)/shard_map/all_to_all | solution.py:315
  105.7 9.8 %gradient.1 = (bf16[8192,128]{1,0:T(8,128)(2,1)}, f32[1,256]{1,0:T(1,128)}) custom-call(bf16[8192,1024]{1,0:T(8,128)(2,1)} %phi.5, bf16[8192,128]{1,0:T(8,128)(2,1)S(1)} %copy-done.1, bf16[128,8,128]{2,1,0:T(8,128)(2,1)S(1)} %all_to_all.20.arrived.loaded, bf16[128,16,128]{2,1,0:T(8,128)(2,1)S(1)} %all_to_all.22.arrived), custom_call_target="tpu_custom_call" | custom-call | tf_op jit(solution)/shard_map/gradient/pallas_call | solution.py:376
  (7 shorter events, 0.0 us)
Async XLA Ops:
  0.6 15.7 %collective-permute-start = (bf16[256,1024]{1,0:T(8,128)(2,1)}, bf16[256,1024]{1,0:T(8,128)(2,1)}, u32[]{:S(2)}, u32[]{:S(2)}) collective-permute-start(bf16[256,1024]{1,0:T(8,128)(2,1)} %refs_0_.3), channel_id=1, source_target_pairs={{0,1},{1,2},{2,3},{3,0},{4,7},{5,4},{6,5},{7,6},{8,9},{9,10},{10,1... | collective-permute-start | bytes 1572872 | tf_op jit(solution)/shard_map/ppermute | solution.py:270
  5.3 10.8 %collective-permute-start.1 = (bf16[128,1024]{1,0:T(8,128)(2,1)S(1)}, bf16[128,1024]{1,0:T(8,128)(2,1)S(1)}, u32[]{:S(2)}, u32[]{:S(2)}) collective-permute-start(bf16[128,1024]{1,0:T(8,128)(2,1)S(1)} %constant_dynamic-slice_fusion), channel_id=1, source_target_pairs={{0,2},{1,3},{2,0},{3,1},{4,6},{5,7},{6,4},{7,5},{8,10},{9,11},{10,... | collective-permute-start | bytes 786440 | tf_op jit(solution)/shard_map/ppermute | solution.py:270
  5.7 1.6 %copy-start = (bf16[8192,128]{1,0:T(8,128)(2,1)S(1)}, bf16[8192,128]{1,0:T(8,128)(2,1)}, u32[]{:S(2)}) copy-start(bf16[8192,128]{1,0:T(8,128)(2,1)} %y.5) | copy-start | bytes 6291460
  7.3 0.7 copy-start.8
  8.0 0.7 copy-start.9
  8.6 32.9 %copy-start.2 = (bf16[256,1024]{1,0:T(8,128)(2,1)S(1)}, bf16[256,1024]{1,0:T(8,128)(2,1)}, u32[]{:S(2)}) copy-start(bf16[256,1024]{1,0:T(8,128)(2,1)} %refs_0_.3) | copy-start | bytes 1572868
  8.6 32.9 %copy-start.7 = (s32[8,8]{1,0:T(8,128)S(1)}, s32[8,8]{1,0:T(8,128)}, u32[]{:S(2)}) copy-start(s32[8,8]{1,0:T(8,128)} %pattern.3) | copy-start | bytes 772
  15.3 0.8 copy-start.3
  16.1 43.9 %copy-start.1 = (bf16[8192,128]{1,0:T(8,128)(2,1)S(1)}, bf16[8192,128]{1,0:T(8,128)(2,1)}, u32[]{:S(2)}) copy-start(bf16[8192,128]{1,0:T(8,128)(2,1)} %y.5) | copy-start | bytes 6291460
  16.3 25.2 %collective-permute-start.2 = (bf16[256,1024]{1,0:T(8,128)(2,1)}, bf16[256,1024]{1,0:T(8,128)(2,1)}, u32[]{:S(2)}, u32[]{:S(2)}) collective-permute-start(bf16[256,1024]{1,0:T(8,128)(2,1)} %collective-permute-done.refs_1_), channel_id=1, source_target_pairs={{0,4},{1,5},{2,6},{3,7},{4,0},{5,1},{6,2},{7,3},{8,12},{9,13},{10,... | collective-permute-start | bytes 1572872 | tf_op jit(solution)/shard_map/ppermute | solution.py:270
  19.7 21.9 %all-to-all-start = ((bf16[128,16,128]{2,1,0:T(8,128)(2,1)}), bf16[128,16,128]{2,1,0:T(8,128)(2,1)S(1)}, u32[]{:S(2)}, u32[]{:S(2)}) async-start(bf16[128,16,128]{2,1,0:T(8,128)(2,1)} %copy-done.3), calls=%async_computation | async-start | bytes 1048576 | tf_op jit(solution)/shard_map/all_to_all | solution.py:315
  27.4 2.3 %collective-permute-start.3 = (bf16[128,1024]{1,0:T(8,128)(2,1)S(1)}, bf16[128,1024]{1,0:T(8,128)(2,1)S(1)}, u32[]{:S(2)}, u32[]{:S(2)}) collective-permute-start(bf16[128,1024]{1,0:T(8,128)(2,1)S(1)} %collective-permute-done.1.refs_2_), channel_id=1, source_target_pairs={{0,4},{1,5},{2,6},{3,7},{4,0},{5,1},{6,2},{7,3},{8,12},{9,13},{10,... | collective-permute-start | bytes 786440 | tf_op jit(solution)/shard_map/ppermute | solution.py:270
  29.7 0.7 copy-start.4
  41.6 1.0 copy-start.5
  60.0 25.2 %copy-start.6 = (bf16[128,1024]{1,0:T(8,128)(2,1)S(1)}, bf16[128,1024]{1,0:T(8,128)(2,1)}, u32[]{:S(2)}) copy-start(bf16[128,1024]{1,0:T(8,128)(2,1)} %copy-done.4) | copy-start | bytes 786436

commit v3 on v2

--- a/solution.py
+++ b/solution.py
@@ -10,7 +10,7 @@
 BLOCK = 128
 LANES = 128
 TILE_ROWS = 1024
-VMEM_LIMIT = 48 * 1024 * 1024
+MIB = 1024 * 1024
 ALL = ("region", "basis")
 F32 = jnp.float32
 BF16 = jnp.bfloat16
@@ -43,22 +43,14 @@
 
 
 def start_mixing(pieces, mixing, sems):
-    own, near, far, near_other, far_other = pieces
-    share, part = own.shape[0], far.shape[0]
+    share = pieces[0].shape[0]
     owner = lax.axis_index("basis")
     core = lax.rem(lax.axis_index("region"), 2)
-    across = lax.rem(owner + 2, OWNERS) * share
-    starts = (
-        owner * share,
-        lax.rem(owner + 3 + 2 * core, OWNERS) * share,
-        across + core * part,
-        lax.rem(owner + 1 + 2 * core, OWNERS) * share,
-        across + (1 - core) * part,
-    )
+    shifts = (0, 3 + 2 * core, 1 + 2 * core, 2)
     copies = []
-    for k, (piece, start) in enumerate(zip(pieces, starts)):
-        at = pl.ds(pl.multiple_of(start, part), piece.shape[0])
-        copies.append(pltpu.make_async_copy(piece, mixing.at[at], sems.at[k]))
+    for k, (piece, shift) in enumerate(zip(pieces, shifts)):
+        start = pl.multiple_of(lax.rem(owner + shift, OWNERS) * share, share)
+        copies.append(pltpu.make_async_copy(piece, mixing.at[pl.ds(start, share)], sems.at[k]))
         copies[-1].start()
     return copies
 
@@ -91,8 +83,29 @@
         ].astype(BF16)
 
 
-def summary_kernel(tile, phi, y, rates, loads, message, phi_here, y_here, total, spread, sems):
+def summary_kernel(
+    tile,
+    phi,
+    y,
+    rates_away,
+    loads_away,
+    message,
+    phi_here,
+    y_here,
+    rates,
+    loads,
+    total,
+    spread,
+    sems,
+    small_sems,
+):
+    small = (
+        pltpu.make_async_copy(rates_away, rates, small_sems.at[0]),
+        pltpu.make_async_copy(loads_away, loads, small_sems.at[1]),
+    )
     chunks = start_chunks(tile, ((y, y_here), (phi, phi_here)), sems)
+    for copy in small:
+        copy.start()
     for i, (at, copies) in enumerate(chunks):
         wait_all(copies)
         product = jnp.dot(y_here[at, :].T, phi_here[at, :], preferred_element_type=F32)
@@ -101,6 +114,7 @@
         else:
             total[...] += product
     store_by_trait(total[...], spread, message)
+    wait_all(small)
     groups = total.shape[1] // LANES
     pieces = []
     for vector in (rates, loads):
@@ -145,10 +159,13 @@
             load_rows.append(wide[at : at + 1, :] + wide[at + halves : at + halves + 1, :])
     loads[...] = jnp.concatenate(load_rows, axis=0)
     wait_all(copies)
-    for s in range(groups):
-        kept = keep(summary, [pattern[s, k] for k in range(groups)])
-        product = contract_lanes(kept, mixing[s * LANES : (s + 1) * LANES, :])
-        tiles[pl.ds(s, count, stride=groups), :] = product + summary[s]
+    for s in range(0, groups, 2):
+        kept = [keep(summary, [pattern[t, k] for k in range(groups)]) for t in (s, s + 1)]
+        product = contract_lanes(
+            jnp.concatenate(kept, axis=0), mixing[s * LANES : (s + 2) * LANES, :]
+        )
+        tiles[pl.ds(s, count, stride=groups), :] = product[:count, :LANES] + summary[s]
+        tiles[pl.ds(s + 1, count, stride=groups), :] = product[count:, LANES:] + summary[s + 1]
     carried = jnp.zeros((groups, LANES), F32)
     scale = loads[...]
     for r in range(count):
@@ -160,13 +177,16 @@
 
 
 def residual_kernel(
-    tile, phi, y, arrived, message, phi_here, y_here, weights, total, spread, sems
+    tile, phi, y, arrived, message, kept, phi_here, y_here, weights, total, spread, sems
 ):
     chunks = start_chunks(tile, ((y, y_here), (phi, phi_here)), sems)
+    traits = arrived.shape[0]
     load_by_trait(arrived, spread, weights, 0)
+    weights[traits:, :] = weights[:traits, :]
+    kept[...] = weights[:traits, :]
     for i, (at, copies) in enumerate(chunks):
         wait_all(copies)
-        fitted = contract_lanes(weights[...], phi_here[at, :])
+        fitted = contract_lanes(weights[...], phi_here[at, :])[:traits]
         residual = (fitted - y_here[at, :].T.astype(F32)).astype(BF16)
         product = jnp.dot(residual, phi_here[at, :], preferred_element_type=F32)
         if i == 0:
@@ -208,12 +228,15 @@
         tiles[pl.ds(s, count, stride=groups), :].astype(BF16).astype(F32) for s in range(groups)
     ]
     wait_all(copies)
-    for s in range(groups):
-        kept = keep(blocks, [pattern[k, s] for k in range(groups)])
+    for s in range(0, groups, 2):
+        kept = [keep(blocks, [pattern[k, t] for k in range(groups)]) for t in (s, s + 1)]
         product = jnp.dot(
-            kept, mixing[:, s * LANES : (s + 1) * LANES], preferred_element_type=F32
+            jnp.concatenate(kept, axis=0),
+            mixing[:, s * LANES : (s + 2) * LANES],
+            preferred_element_type=F32,
         )
-        tiles[pl.ds(s, count, stride=groups), :] = product + blocks[s]
+        tiles[pl.ds(s, count, stride=groups), :] = product[:count, :LANES] + blocks[s]
+        tiles[pl.ds(s + 1, count, stride=groups), :] = product[count:, LANES:] + blocks[s + 1]
     for r in range(count):
         back = tiles[r * groups : (r + 1) * groups, :].astype(BF16)
         for b in range(owners):
@@ -240,12 +263,7 @@
     traits = loaded.shape[0]
     groups = weights.shape[1] // LANES
     load_by_trait(arrived, spread, weights, 0)
-    load_by_trait(loaded, spread, weights, traits)
-    tail = jnp.sum(arrived[:, groups : 2 * groups, :].astype(F32), axis=0)
-    for h in range(halves):
-        slope[:, h * LANES : (h + 1) * LANES] = (
-            tail[h : h + 1, :] + tail[halves + h : halves + h + 1, :]
-        )
+    weights[traits:, :] = loaded[...]
     stores = []
     for i, (at, copies) in enumerate(chunks):
         wait_all(copies)
@@ -254,34 +272,31 @@
         out_here[at, :] = (both[:traits] - residual.astype(F32)).astype(BF16).T
         stores.append(pltpu.make_async_copy(out_here.at[at], out.at[at], sems.at[2, i]))
         stores[-1].start()
+    tail = jnp.sum(arrived[:, groups : 2 * groups, :].astype(F32), axis=0)
+    for h in range(halves):
+        slope[:, h * LANES : (h + 1) * LANES] = (
+            tail[h : h + 1, :] + tail[halves + h : halves + h + 1, :]
+        )
     wait_all(stores)
 
 
-def mixing_pieces(mixing):
-    regions = lax.axis_size("region")
-    part = mixing.shape[0] // 2
-    core = lax.rem(lax.axis_index("region"), 2)
-    half = lax.dynamic_slice_in_dim(mixing, core * part, part, 0)
-
-    def move(value, target):
-        pairs = [
-            (r * OWNERS + b, target(r, b)) for r in range(regions) for b in range(OWNERS)
-        ]
-        return lax.ppermute(value, ALL, pairs)
-
-    def beside(r, b):
-        return r * OWNERS + (b + 1 + 2 * (r % 2)) % OWNERS
-
-    def across(r, b):
-        return r * OWNERS + (b + 2) % OWNERS
-
-    def other_core(r, b):
-        return (r ^ 1) * OWNERS + b
-
-    def swap(near, far):
-        return mixing, near, far, move(near, other_core), move(far, other_core)
-
-    return (move(mixing, beside), move(half, across)), swap
+def permute(value, target):
+    pairs = []
+    for r in range(lax.axis_size("region")):
+        for b in range(OWNERS):
+            to_r, to_b = target(r, b)
+            pairs.append((r * OWNERS + b, to_r * OWNERS + to_b % OWNERS))
+    return lax.ppermute(value, ALL, pairs)
+
+
+def near_shard(mixing):
+    return permute(mixing, lambda r, b: (r, b + 1 + 2 * (r % 2)))
+
+
+def other_shards(near):
+    swapped = permute(near, lambda r, b: (r ^ 1, b))
+    across = permute(near, lambda r, b: (r ^ 1, b + 1 + 2 * (r % 2)))
+    return swapped, across
 
 
 def shards(count, observations, basis_values, mixing, pattern, decays, loadings):
@@ -293,12 +308,11 @@
     halves = share // LANES
     tile = min(TILE_ROWS, rows)
     chunks = rows // tile
-    fetched, swap = mixing_pieces(mixing)
+    near = near_shard(mixing)
 
     hbm = pl.BlockSpec(memory_space=pl.ANY)
     vmem = pl.BlockSpec(memory_space=pltpu.VMEM)
     smem = pl.BlockSpec(memory_space=pltpu.SMEM)
-    params = pltpu.CompilerParams(vmem_limit_bytes=VMEM_LIMIT)
     phi_here = pltpu.VMEM((rows, width), BF16)
     y_here = pltpu.VMEM((rows, traits), BF16)
     total = pltpu.VMEM((traits, width), F32)
@@ -311,20 +325,32 @@
     def sems(*shape):
         return pltpu.SemaphoreType.DMA(shape)
 
+    def limit(mebibytes):
+        return pltpu.CompilerParams(vmem_limit_bytes=mebibytes * MIB)
+
     def exchange(value):
         return lax.all_to_all(value, ALL, 0, 0, tiled=True)
 
     sums = pl.pallas_call(
         functools.partial(summary_kernel, tile),
-        in_specs=[hbm, hbm, vmem, vmem],
+        in_specs=[hbm] * 4,
         out_specs=vmem,
         out_shape=long,
-        scratch_shapes=[phi_here, y_here, total, spread, sems(2, chunks)],
-        compiler_params=params,
+        scratch_shapes=[
+            phi_here,
+            y_here,
+            pltpu.VMEM((1, share), F32),
+            pltpu.VMEM((1, share), F32),
+            total,
+            spread,
+            sems(2, chunks),
+            sems(2),
+        ],
+        compiler_params=limit(60),
         name="summary",
     )(basis_values, observations, decays, loadings[None, :])
-    sums, fetched = lax.optimization_barrier((sums, fetched))
-    pieces = swap(*fetched)
+    sums, near = lax.optimization_barrier((sums, near))
+    pieces = (mixing, near) + other_shards(near)
     sums = exchange(sums)
     loaded, previous, rates, loads = pl.pallas_call(
         functools.partial(forward_kernel, count),
@@ -342,24 +368,24 @@
             tiles,
             sems(len(pieces)),
         ],
-        compiler_params=params,
+        compiler_params=limit(16),
         name="forward",
     )(sums, pattern, *pieces)
     loaded = exchange(loaded)
-    pulled = pl.pallas_call(
+    pulled, loaded = pl.pallas_call(
         functools.partial(residual_kernel, tile),
         in_specs=[hbm, hbm, vmem],
-        out_specs=vmem,
-        out_shape=short,
+        out_specs=(vmem, vmem),
+        out_shape=(short, jax.ShapeDtypeStruct((traits, width), BF16)),
         scratch_shapes=[
             phi_here,
             y_here,
-            pltpu.VMEM((traits, width), BF16),
+            pltpu.VMEM((2 * traits, width), BF16),
             total,
             spread,
             sems(2, chunks),
         ],
-        compiler_params=params,
+        compiler_params=limit(44),
         name="residual",
     )(basis_values, observations, loaded)
     pulled = exchange(pulled)
@@ -369,7 +395,7 @@
         out_specs=vmem,
         out_shape=long,
         scratch_shapes=[mixing_here, tiles, sems(len(pieces))],
-        compiler_params=params,
+        compiler_params=limit(16),
         name="backward",
     )(pulled, pattern, previous, rates, loads, *pieces)
     back = exchange(back)
@@ -389,7 +415,7 @@
             spread,
             sems(3, chunks),
         ],
-        compiler_params=params,
+        compiler_params=limit(44),
         name="gradient",
     )(basis_values, observations, loaded, back)
     return obs_grad, slope

time: 116 us -> 107 us (0.922)
  blocking collectives: 47.5 us -> 70.1 us
  waiting for transfers between devices: 12.5 us -> 0.01 us
  starting transfers between devices: 16.3 us -> 5.52 us
  local copies, waits for them, and re-layouts: 6.42 us -> 0.01 us
  Pallas kernels: 32 us -> 30.6 us
    all_to_all x3 -> x4, blocking collectives: 47.5 us -> 70.1 us  [exchange(): return lax.all_to_all(value, ALL, 0, 0, tiled=True)]
    all_to_all x1 -> x0, waiting for transfers between devices: 11.1 us -> none  [exchange(): return lax.all_to_all(value, ALL, 0, 0, tiled=True)]
    all_to_all x1 -> x0, starting transfers between devices: 7.76 us -> none  [exchange(): return lax.all_to_all(value, ALL, 0, 0, tiled=True)]
    unnamed x20 -> x6, local copies, waits for them, and re-layouts: 5.42 us -> 0.01 us
    ppermute x4 -> x3, starting transfers between devices: 8.55 us -> 5.52 us  [permute(): return lax.ppermute(value, ALL, pairs)]
    pallas_call x1, Pallas kernels: 6.6 us -> 8.03 us  [shards(): pl.pallas_call(functools.partial(summary_kernel, tile), in_specs=[hbm] *...]
    ppermute x4 -> x3, waiting for transfers between devices: 1.43 us -> 0.01 us  [permute(): return lax.ppermute(value, ALL, pairs)]
    pallas_call x1, Pallas kernels: 2.7 us -> 1.49 us  [shards(): pl.pallas_call(functools.partial(backward_kernel, count, traits), in_spec...]
  transfers between devices with their start and end apart: 5 -> 3, of which waited for: 3 -> 0; matrix products, arithmetic and copies ran while one was open for 1% -> 0% of each run, Pallas kernels for 6% -> 8%
where the time goes in v3:
time: 107 us
  blocking collectives  70.1 us (66%)
  Pallas kernels  30.6 us (29%)
  starting transfers between devices  5.52 us (5%)
    all_to_all x4, blocking collectives, exchange(): return lax.all_to_all(value, ALL, 0, 0, tiled=True)  70.1 us
    pallas_call x1, Pallas kernels, shards(): pl.pallas_call(functools.partial(gradient_kernel, tile, halves), in_specs...  9.8 us
    pallas_call x1, Pallas kernels, shards(): pl.pallas_call(functools.partial(residual_kernel, tile), in_specs=[hbm, h...  9.17 us
    pallas_call x1, Pallas kernels, shards(): pl.pallas_call(functools.partial(summary_kernel, tile), in_specs=[hbm] *...  8.03 us
    ppermute x3, starting transfers between devices, permute(): return lax.ppermute(value, ALL, pairs)  5.52 us
    pallas_call x1, Pallas kernels, shards(): pl.pallas_call(functools.partial(forward_kernel, count), in_specs=[vmem,...  2.15 us
  transfers between devices with their start and end apart: 3, of which 0 were waited for; matrix products, arithmetic and copies ran while one was open for 0% of the time, Pallas kernels for 8%

profile of v3, /device:TPU:1, one launch (start us, length us, event | category | flops | bytes accessed | tf_op | source)
XLA Modules:
  0.0 107.1 jit_solution(7458032586223526560)
XLA Ops:
  0.6 3.6 %collective-permute-start = (bf16[256,1024]{1,0:T(8,128)(2,1)}, bf16[256,1024]{1,0:T(8,128)(2,1)S(1)}, u32[]{:S(2)}, u32[]{:S(2)}) collective-permute-start(bf16[256,1024]{1,0:T(8,128)(2,1)} %refs_0_.3), channel_id=1, source_target_pairs={{0,1},{1,2},{2,3},{3,0},{4,7},{5,4},{6,5},{7,6},{8,9},{9,10},{10,1... | collective-permute-start | bytes 1572872 | tf_op jit(solution)/shard_map/ppermute | solution.py:289
  4.3 0.0 copy-start.1
  4.3 0.0 copy-start.2
  4.3 8.0 %summary.1 = bf16[128,16,128]{2,1,0:T(8,128)(2,1)} custom-call(bf16[8192,1024]{1,0:T(8,128)(2,1)} %phi.5, bf16[8192,128]{1,0:T(8,128)(2,1)} %y.5, f32[1,256]{1,0:T(1,128)} %rates_away.1, f32[1,256]{1,0:T(1,128)} %bitcast.1), custom_call_target="tpu_custom_call" | custom-call | tf_op jit(solution)/shard_map/summary/pallas_call | solution.py:334
  12.3 0.0 copy-start
  12.3 0.0 collective-permute-done.refs_1_
  12.3 1.9 %collective-permute-start.2 = (bf16[256,1024]{1,0:T(8,128)(2,1)S(1)}, bf16[256,1024]{1,0:T(8,128)(2,1)S(1)}, u32[]{:S(2)}, u32[]{:S(2)}) collective-permute-start(bf16[256,1024]{1,0:T(8,128)(2,1)S(1)} %collective-permute-done.refs_1_), channel_id=1, source_target_pairs={{0,5},{1,6},{2,7},{3,4},{4,3},{5,0},{6,1},{7,2},{8,13},{9,14},{10,... | collective-permute-start | bytes 1572872 | tf_op jit(solution)/shard_map/ppermute | solution.py:289
  14.2 0.0 collective-permute-start.1
  14.2 22.6 %all_to_all.20.message = bf16[128,16,128]{2,1,0:T(8,128)(2,1)S(1)} all-to-all(bf16[128,16,128]{2,1,0:T(8,128)(2,1)} %summary.1), channel_id=1, replica_groups=mesh['region'=32,'basis'=4] {'region','basis'}, dimensions={0} | all-to-all | bytes 1048576 | tf_op jit(solution)/shard_map/all_to_all | solution.py:332
  36.8 0.0 collective-permute-done.2.refs_3_
  36.8 0.0 collective-permute-done.1.refs_2_
  36.8 0.0 copy-done.1
  36.8 0.0 copy-done.2
  36.8 2.2 %forward.1 = (bf16[128,8,128]{2,1,0:T(8,128)(2,1)S(1)}, f32[32,8,128]{2,1,0:T(8,128)S(1)}, f32[32,8,128]{2,1,0:T(8,128)S(1)}, f32[8,128]{1,0:T(8,128)S(1)}) custom-call(bf16[128,16,128]{2,1,0:T(8,128)(2,1)S(1)} %all_to_all.20.message, s32[8,8]{1,0:T(8,128)S(1)} %copy-done.2, bf16[256,1024]{1,0:T(8,128)(2,1)S(1)} %copy-done.1, ...), custom_call_target="tpu_custom_call" | custom-call | tf_op jit(solution)/shard_map/forward/pallas_call | solution.py:355
  39.0 14.7 %all_to_all.21.arrived = bf16[128,8,128]{2,1,0:T(8,128)(2,1)S(1)} all-to-all(bf16[128,8,128]{2,1,0:T(8,128)(2,1)S(1)} %get-tuple-element.12), channel_id=1, replica_groups=mesh['region'=32,'basis'=4] {'region','basis'}, dimensions={0} | all-to-all | bytes 524288 | tf_op jit(solution)/shard_map/all_to_all | solution.py:332
  53.7 0.0 copy-done
  53.7 9.2 %residual.1 = (bf16[128,8,128]{2,1,0:T(8,128)(2,1)S(1)}, bf16[128,1024]{1,0:T(8,128)(2,1)S(1)}) custom-call(bf16[8192,1024]{1,0:T(8,128)(2,1)} %phi.5, bf16[8192,128]{1,0:T(8,128)(2,1)S(1)} %copy-done, bf16[128,8,128]{2,1,0:T(8,128)(2,1)S(1)} %all_to_all.21.arrived), custom_call_target="tpu_custom_call" | custom-call | tf_op jit(solution)/shard_map/residual/pallas_call | solution.py:375
  62.9 15.0 %all_to_all.22.message = bf16[128,8,128]{2,1,0:T(8,128)(2,1)S(1)} all-to-all(bf16[128,8,128]{2,1,0:T(8,128)(2,1)S(1)} %get-tuple-element.14), channel_id=1, replica_groups=mesh['region'=32,'basis'=4] {'region','basis'}, dimensions={0} | all-to-all | bytes 524288 | tf_op jit(solution)/shard_map/all_to_all | solution.py:332
  77.9 1.5 %backward.1 = bf16[128,16,128]{2,1,0:T(8,128)(2,1)S(1)} custom-call(bf16[128,8,128]{2,1,0:T(8,128)(2,1)S(1)} %all_to_all.22.message, s32[8,8]{1,0:T(8,128)S(1)} %copy-done.2, f32[32,8,128]{2,1,0:T(8,128)S(1)} %get-tuple-element.15.previous, f32[32,8,128]{2,1,0:T(8,128)S(1)} %get-tuple-element.16.rates, f32[8,128]{1,0:T(8,128)S(1)} %get-tuple-element.17.loads, ...), custom_call_target="tpu_custom_call" | custom-call | tf_op jit(solution)/shard_map/backward/pallas_call | solution.py:392
  79.4 17.8 %all_to_all.23.arrived = bf16[128,16,128]{2,1,0:T(8,128)(2,1)S(1)} all-to-all(bf16[128,16,128]{2,1,0:T(8,128)(2,1)S(1)} %backward.1), channel_id=1, replica_groups=mesh['region'=32,'basis'=4] {'region','basis'}, dimensions={0} | all-to-all | bytes 1048576 | tf_op jit(solution)/shard_map/all_to_all | solution.py:332
  97.2 9.8 %gradient.1 = (bf16[8192,128]{1,0:T(8,128)(2,1)}, f32[1,256]{1,0:T(1,128)}) custom-call(bf16[8192,1024]{1,0:T(8,128)(2,1)} %phi.5, bf16[8192,128]{1,0:T(8,128)(2,1)S(1)} %copy-done, bf16[128,1024]{1,0:T(8,128)(2,1)S(1)} %get-tuple-element.13.loaded, bf16[128,16,128]{2,1,0:T(8,128)(2,1)S(1)} %all_to_all.23.arrived), custom_call_target="tpu_custom_call" | custom-call | tf_op jit(solution)/shard_map/gradient/pallas_call | solution.py:402
Async XLA Ops:
  0.6 11.7 %collective-permute-start = (bf16[256,1024]{1,0:T(8,128)(2,1)}, bf16[256,1024]{1,0:T(8,128)(2,1)S(1)}, u32[]{:S(2)}, u32[]{:S(2)}) collective-permute-start(bf16[256,1024]{1,0:T(8,128)(2,1)} %refs_0_.3), channel_id=1, source_target_pairs={{0,1},{1,2},{2,3},{3,0},{4,7},{5,4},{6,5},{7,6},{8,9},{9,10},{10,1... | collective-permute-start | bytes 1572872 | tf_op jit(solution)/shard_map/ppermute | solution.py:289
  4.3 32.6 %copy-start.1 = (bf16[256,1024]{1,0:T(8,128)(2,1)S(1)}, bf16[256,1024]{1,0:T(8,128)(2,1)}, u32[]{:S(2)}) copy-start(bf16[256,1024]{1,0:T(8,128)(2,1)} %refs_0_.3) | copy-start | bytes 1572868
  4.3 32.6 %copy-start.2 = (s32[8,8]{1,0:T(8,128)S(1)}, s32[8,8]{1,0:T(8,128)}, u32[]{:S(2)}) copy-start(s32[8,8]{1,0:T(8,128)} %pattern.3) | copy-start | bytes 772
  12.3 41.4 %copy-start = (bf16[8192,128]{1,0:T(8,128)(2,1)S(1)}, bf16[8192,128]{1,0:T(8,128)(2,1)}, u32[]{:S(2)}) copy-start(bf16[8192,128]{1,0:T(8,128)(2,1)} %y.5) | copy-start | bytes 6291460
  12.3 24.5 %collective-permute-start.2 = (bf16[256,1024]{1,0:T(8,128)(2,1)S(1)}, bf16[256,1024]{1,0:T(8,128)(2,1)S(1)}, u32[]{:S(2)}, u32[]{:S(2)}) collective-permute-start(bf16[256,1024]{1,0:T(8,128)(2,1)S(1)} %collective-permute-done.refs_1_), channel_id=1, source_target_pairs={{0,5},{1,6},{2,7},{3,4},{4,3},{5,0},{6,1},{7,2},{8,13},{9,14},{10,... | collective-permute-start | bytes 1572872 | tf_op jit(solution)/shard_map/ppermute | solution.py:289
  14.2 22.6 %collective-permute-start.1 = (bf16[256,1024]{1,0:T(8,128)(2,1)S(1)}, bf16[256,1024]{1,0:T(8,128)(2,1)S(1)}, u32[]{:S(2)}, u32[]{:S(2)}) collective-permute-start(bf16[256,1024]{1,0:T(8,128)(2,1)S(1)} %collective-permute-done.refs_1_), channel_id=1, source_target_pairs={{0,4},{1,5},{2,6},{3,7},{4,0},{5,1},{6,2},{7,3},{8,12},{9,13},{10,... | collective-permute-start | bytes 1572872 | tf_op jit(solution)/shard_map/ppermute | solution.py:289

commit v4 on v3

--- a/solution.py
+++ b/solution.py
@@ -15,6 +15,8 @@
 F32 = jnp.float32
 BF16 = jnp.bfloat16
 OWNERS = 4
+PART_ROWS = 4
+PARTS = 3
 
 
 def split(value):
@@ -22,11 +24,12 @@
     return high, (value - high.astype(F32)).astype(BF16)
 
 
-def start_chunks(tile, pairs, sems):
-    rows = pairs[0][0].shape[0]
+def start_chunks(sizes, pairs, sems):
     chunks = []
-    for i in range(rows // tile):
-        at = pl.ds(i * tile, tile)
+    start = 0
+    for i, size in enumerate(sizes):
+        at = pl.ds(start, size)
+        start += size
         copies = [
             pltpu.make_async_copy(source.at[at], target.at[at], sems.at[k, i])
             for k, (source, target) in enumerate(pairs)
@@ -42,17 +45,10 @@
         copy.wait()
 
 
-def start_mixing(pieces, mixing, sems):
-    share = pieces[0].shape[0]
+def piece_blocks():
     owner = lax.axis_index("basis")
     core = lax.rem(lax.axis_index("region"), 2)
-    shifts = (0, 3 + 2 * core, 1 + 2 * core, 2)
-    copies = []
-    for k, (piece, shift) in enumerate(zip(pieces, shifts)):
-        start = pl.multiple_of(lax.rem(owner + shift, OWNERS) * share, share)
-        copies.append(pltpu.make_async_copy(piece, mixing.at[pl.ds(start, share)], sems.at[k]))
-        copies[-1].start()
-    return copies
+    return [2 * lax.rem(owner + shift, OWNERS) for shift in (0, 3 + 2 * core, 1 + 2 * core, 2)]
 
 
 def keep(blocks, present):
@@ -73,18 +69,22 @@
     message[:, 0:groups, :] = spread[...].reshape(traits, groups, LANES).astype(BF16)
 
 
-def load_by_trait(message, spread, target, at):
+def gather_traits(spread, target, traits, groups):
+    for s in range(groups):
+        target[0:traits, s * LANES : (s + 1) * LANES] = spread[
+            pl.ds(s, traits, stride=groups), :
+        ].astype(BF16)
+
+
+def load_by_trait(message, spread, target):
     traits = message.shape[0]
     groups = target.shape[1] // LANES
-    spread[...] = message[:, 0:groups, :].astype(F32).reshape(traits * groups, LANES)
-    for s in range(groups):
-        target[at : at + traits, s * LANES : (s + 1) * LANES] = spread[
-            pl.ds(s, traits, stride=groups), :
-        ].astype(BF16)
+    spread[...] = message[...].astype(F32).reshape(traits * groups, LANES)
+    gather_traits(spread, target, traits, groups)
 
 
 def summary_kernel(
-    tile,
+    sizes,
     phi,
     y,
     rates_away,
@@ -103,7 +103,7 @@
         pltpu.make_async_copy(rates_away, rates, small_sems.at[0]),
         pltpu.make_async_copy(loads_away, loads, small_sems.at[1]),
     )
-    chunks = start_chunks(tile, ((y, y_here), (phi, phi_here)), sems)
+    chunks = start_chunks(sizes, ((y, y_here), (phi, phi_here)), sems)
     for copy in small:
         copy.start()
     for i, (at, copies) in enumerate(chunks):
@@ -128,11 +128,10 @@
 
 
 def forward_kernel(count, message, pattern, *refs):
-    *pieces, reply, previous, rates, loads, mixing, wide, tiles, sems = refs
-    copies = start_mixing(pieces, mixing, sems)
+    *pieces, reply, previous, rates, loads, sums, wide, tiles = refs
     devices, rows, _ = message.shape
     owners = devices // count
-    groups = mixing.shape[0] // LANES
+    groups = pieces[0].shape[1] // LANES
     halves = groups // owners
     wide[...] = message[...].astype(F32).reshape(devices * rows, LANES)
     step = owners * rows
@@ -146,6 +145,7 @@
         for b in range(1, owners):
             block = block + column(b * rows + s)
         summary.append(block.astype(BF16).astype(F32))
+        sums[s] = summary[s]
     for b in range(owners):
         for h in range(halves):
             at = b * rows + groups + h
@@ -158,14 +158,11 @@
             at = b * rows + groups + 2 * halves + h
             load_rows.append(wide[at : at + 1, :] + wide[at + halves : at + halves + 1, :])
     loads[...] = jnp.concatenate(load_rows, axis=0)
-    wait_all(copies)
-    for s in range(0, groups, 2):
+    for piece, s in zip(pieces, piece_blocks()):
         kept = [keep(summary, [pattern[t, k] for k in range(groups)]) for t in (s, s + 1)]
-        product = contract_lanes(
-            jnp.concatenate(kept, axis=0), mixing[s * LANES : (s + 2) * LANES, :]
-        )
-        tiles[pl.ds(s, count, stride=groups), :] = product[:count, :LANES] + summary[s]
-        tiles[pl.ds(s + 1, count, stride=groups), :] = product[count:, LANES:] + summary[s + 1]
+        product = contract_lanes(jnp.concatenate(kept, axis=0), piece[...])
+        tiles[pl.ds(s, count, stride=groups), :] = product[:count, :LANES] + sums[s]
+        tiles[pl.ds(s + 1, count, stride=groups), :] = product[count:, LANES:] + sums[s + 1]
     carried = jnp.zeros((groups, LANES), F32)
     scale = loads[...]
     for r in range(count):
@@ -176,18 +173,16 @@
             reply[r * owners + b] = value
 
 
-def residual_kernel(
-    tile, phi, y, arrived, message, kept, phi_here, y_here, weights, total, spread, sems
-):
-    chunks = start_chunks(tile, ((y, y_here), (phi, phi_here)), sems)
+def residual_kernel(sizes, phi, y, arrived, message, kept, phi_here, weights, total, spread, sems):
+    chunks = start_chunks(sizes, ((phi, phi_here),), sems)
     traits = arrived.shape[0]
-    load_by_trait(arrived, spread, weights, 0)
+    load_by_trait(arrived, spread, weights)
     weights[traits:, :] = weights[:traits, :]
     kept[...] = weights[:traits, :]
     for i, (at, copies) in enumerate(chunks):
         wait_all(copies)
         fitted = contract_lanes(weights[...], phi_here[at, :])[:traits]
-        residual = (fitted - y_here[at, :].T.astype(F32)).astype(BF16)
+        residual = (fitted - y[at, :].T.astype(F32)).astype(BF16)
         product = jnp.dot(residual, phi_here[at, :], preferred_element_type=F32)
         if i == 0:
             total[...] = product
@@ -197,11 +192,10 @@
 
 
 def backward_kernel(count, traits, message, pattern, previous, rates, loads, *refs):
-    *pieces, reply, mixing, tiles, sems = refs
-    copies = start_mixing(pieces, mixing, sems)
+    *pieces, reply, tiles = refs
     devices = message.shape[0]
     owners = devices // count
-    groups = mixing.shape[0] // LANES
+    groups = pieces[0].shape[1] // LANES
     halves = groups // owners
     scale = loads[...]
     adjoint = jnp.zeros((groups, LANES), F32)
@@ -220,59 +214,62 @@
         high, low = high.astype(F32), low.astype(F32)
         for b in range(owners):
             mine = slice(b * halves, (b + 1) * halves)
-            tail = jnp.concatenate(
-                [high[mine], low[mine], jnp.zeros((groups - 2 * halves, LANES), F32)], axis=0
+            tail = jnp.concatenate([high[mine], low[mine]], axis=0)
+            reply[(r * owners + b) * PARTS + PARTS - 1] = tail.astype(BF16)
+    def block(s):
+        return tiles[pl.ds(s, count, stride=groups), :].astype(BF16).astype(F32)
+
+    blocks = [block(s) for s in range(groups)]
+    firsts = piece_blocks()
+    parts = [(block(s), block(s + 1)) for s in firsts]
+    for s in range(0, groups, 2):
+        product = jnp.zeros((2 * count, 2 * LANES), F32)
+        for piece, first, part in zip(pieces, firsts, parts):
+            kept = [keep(part, (pattern[first, t], pattern[first + 1, t])) for t in (s, s + 1)]
+            product += jnp.dot(
+                jnp.concatenate(kept, axis=0),
+                piece[:, s * LANES : (s + 2) * LANES],
+                preferred_element_type=F32,
             )
-            reply[r * owners + b, groups : 2 * groups, :] = tail.astype(BF16)
-    blocks = [
-        tiles[pl.ds(s, count, stride=groups), :].astype(BF16).astype(F32) for s in range(groups)
-    ]
-    wait_all(copies)
-    for s in range(0, groups, 2):
-        kept = [keep(blocks, [pattern[k, t] for k in range(groups)]) for t in (s, s + 1)]
-        product = jnp.dot(
-            jnp.concatenate(kept, axis=0),
-            mixing[:, s * LANES : (s + 2) * LANES],
-            preferred_element_type=F32,
-        )
         tiles[pl.ds(s, count, stride=groups), :] = product[:count, :LANES] + blocks[s]
         tiles[pl.ds(s + 1, count, stride=groups), :] = product[count:, LANES:] + blocks[s + 1]
     for r in range(count):
-        back = tiles[r * groups : (r + 1) * groups, :].astype(BF16)
-        for b in range(owners):
-            reply[r * owners + b, 0:groups, :] = back
+        for part in range(PARTS - 1):
+            at = r * groups + part * PART_ROWS
+            back = tiles[at : at + PART_ROWS, :].astype(BF16)
+            for b in range(owners):
+                reply[(r * owners + b) * PARTS + part] = back
 
 
 def gradient_kernel(
-    tile,
-    halves,
-    phi,
-    y,
-    loaded,
-    arrived,
-    out,
-    slope,
-    phi_here,
-    y_here,
-    out_here,
-    weights,
-    spread,
-    sems,
+    sizes, halves, phi, y, loaded, arrived, out, slope, phi_here, out_here, weights, spread, sent, sems
 ):
-    chunks = start_chunks(tile, ((y, y_here), (phi, phi_here)), sems)
+    chunks = start_chunks(sizes, ((phi, phi_here),), sems)
     traits = loaded.shape[0]
     groups = weights.shape[1] // LANES
-    load_by_trait(arrived, spread, weights, 0)
+    for k in range(traits):
+        for part in range(PARTS - 1):
+            at = k * groups + part * PART_ROWS
+            spread[at : at + PART_ROWS, :] = arrived[k * PARTS + part].astype(F32)
+    gather_traits(spread, weights, traits, groups)
     weights[traits:, :] = loaded[...]
     stores = []
+
+    def finish(i):
+        at = chunks[i][0]
+        both = sent[i % 2, :, 0 : sizes[i]]
+        residual = (both[traits:] - y[at, :].T.astype(F32)).astype(BF16)
+        out_here[at, :] = (both[:traits] - residual.astype(F32)).astype(BF16).T
+        stores.append(pltpu.make_async_copy(out_here.at[at], out.at[at], sems.at[1, i]))
+        stores[-1].start()
+
     for i, (at, copies) in enumerate(chunks):
         wait_all(copies)
-        both = contract_lanes(weights[...], phi_here[at, :])
-        residual = (both[traits:] - y_here[at, :].T.astype(F32)).astype(BF16)
-        out_here[at, :] = (both[:traits] - residual.astype(F32)).astype(BF16).T
-        stores.append(pltpu.make_async_copy(out_here.at[at], out.at[at], sems.at[2, i]))
-        stores[-1].start()
-    tail = jnp.sum(arrived[:, groups : 2 * groups, :].astype(F32), axis=0)
+        sent[i % 2, :, 0 : sizes[i]] = contract_lanes(weights[...], phi_here[at, :])
+        if i > 0:
+            finish(i - 1)
+    finish(len(chunks) - 1)
+    tail = jnp.sum(arrived[pl.ds(PARTS - 1, traits, stride=PARTS)].astype(F32), axis=0)
     for h in range(halves):
         slope[:, h * LANES : (h + 1) * LANES] = (
             tail[h : h + 1, :] + tail[halves + h : halves + h + 1, :]
@@ -307,7 +304,8 @@
     share = decays.shape[1]
     halves = share // LANES
     tile = min(TILE_ROWS, rows)
-    chunks = rows // tile
+    even = (tile,) * (rows // tile)
+    tapered = (tile // 2,) * 2 + even[2:] + (tile // 2,) * 2
     near = near_shard(mixing)
 
     hbm = pl.BlockSpec(memory_space=pl.ANY)
@@ -318,7 +316,6 @@
     total = pltpu.VMEM((traits, width), F32)
     spread = pltpu.VMEM((traits * groups, LANES), F32)
     tiles = pltpu.VMEM((count * groups, LANES), F32)
-    mixing_here = pltpu.VMEM((width, width), BF16)
     short = jax.ShapeDtypeStruct((devices, groups, LANES), BF16)
     long = jax.ShapeDtypeStruct((devices, 2 * groups, LANES), BF16)
 
@@ -332,7 +329,7 @@
         return lax.all_to_all(value, ALL, 0, 0, tiled=True)
 
     sums = pl.pallas_call(
-        functools.partial(summary_kernel, tile),
+        functools.partial(summary_kernel, tapered),
         in_specs=[hbm] * 4,
         out_specs=vmem,
         out_shape=long,
@@ -343,7 +340,7 @@
             pltpu.VMEM((1, share), F32),
             total,
             spread,
-            sems(2, chunks),
+            sems(2, len(tapered)),
             sems(2),
         ],
         compiler_params=limit(60),
@@ -354,7 +351,7 @@
     sums = exchange(sums)
     loaded, previous, rates, loads = pl.pallas_call(
         functools.partial(forward_kernel, count),
-        in_specs=[vmem, smem] + [hbm] * len(pieces),
+        in_specs=[vmem, smem] + [vmem] * len(pieces),
         out_specs=(vmem,) * 4,
         out_shape=(
             short,
@@ -363,27 +360,25 @@
             jax.ShapeDtypeStruct((groups, LANES), F32),
         ),
         scratch_shapes=[
-            mixing_here,
+            pltpu.VMEM((groups, count, LANES), F32),
             pltpu.VMEM((devices * 2 * groups, LANES), F32),
             tiles,
-            sems(len(pieces)),
         ],
         compiler_params=limit(16),
         name="forward",
     )(sums, pattern, *pieces)
     loaded = exchange(loaded)
     pulled, loaded = pl.pallas_call(
-        functools.partial(residual_kernel, tile),
-        in_specs=[hbm, hbm, vmem],
+        functools.partial(residual_kernel, even),
+        in_specs=[hbm, vmem, vmem],
         out_specs=(vmem, vmem),
         out_shape=(short, jax.ShapeDtypeStruct((traits, width), BF16)),
         scratch_shapes=[
             phi_here,
-            y_here,
             pltpu.VMEM((2 * traits, width), BF16),
             total,
             spread,
-            sems(2, chunks),
+            sems(1, len(even)),
         ],
         compiler_params=limit(44),
         name="residual",
@@ -391,17 +386,17 @@
     pulled = exchange(pulled)
     back = pl.pallas_call(
         functools.partial(backward_kernel, count, traits),
-        in_specs=[vmem, smem, vmem, vmem, vmem] + [hbm] * len(pieces),
+        in_specs=[vmem, smem, vmem, vmem, vmem] + [vmem] * len(pieces),
         out_specs=vmem,
-        out_shape=long,
-        scratch_shapes=[mixing_here, tiles, sems(len(pieces))],
+        out_shape=jax.ShapeDtypeStruct((devices * PARTS, PART_ROWS, LANES), BF16),
+        scratch_shapes=[tiles],
         compiler_params=limit(16),
         name="backward",
     )(pulled, pattern, previous, rates, loads, *pieces)
     back = exchange(back)
     obs_grad, slope = pl.pallas_call(
-        functools.partial(gradient_kernel, tile, halves),
-        in_specs=[hbm, hbm, vmem, vmem],
+        functools.partial(gradient_kernel, tapered, halves),
+        in_specs=[hbm, vmem, vmem, vmem],
         out_specs=(hbm, vmem),
         out_shape=(
             jax.ShapeDtypeStruct((rows, traits), BF16),
@@ -410,10 +405,10 @@
         scratch_shapes=[
             phi_here,
             y_here,
-            y_here,
             pltpu.VMEM((2 * traits, width), BF16),
             spread,
-            sems(3, chunks),
+            pltpu.VMEM((2, 2 * traits, tile), F32),
+            sems(2, len(tapered)),
         ],
         compiler_params=limit(44),
         name="gradient",

time: 107 us -> 104 us (0.972)
  Pallas kernels: 30.6 us -> 29 us
  blocking collectives: 70.1 us -> 68.5 us
    all_to_all x4, blocking collectives: 70.1 us -> 68.5 us  [exchange(): return lax.all_to_all(value, ALL, 0, 0, tiled=True)]
where the time goes in v4:
time: 104 us
  blocking collectives  68.5 us (66%)
  Pallas kernels  29 us (28%)
  starting transfers between devices  5.67 us (5%)
    all_to_all x4, blocking collectives, exchange(): return lax.all_to_all(value, ALL, 0, 0, tiled=True)  68.5 us
    pallas_call x1, Pallas kernels, shards(): pl.pallas_call(functools.partial(gradient_kernel, tapered, halves), in_sp...  9.12 us
    pallas_call x1, Pallas kernels, shards(): pl.pallas_call(functools.partial(residual_kernel, even), in_specs=[hbm, v...  9.09 us
    pallas_call x1, Pallas kernels, shards(): pl.pallas_call(functools.partial(summary_kernel, tapered), in_specs=[hbm]...  7.88 us
    ppermute x3, starting transfers between devices, permute(): return lax.ppermute(value, ALL, pairs)  5.67 us
  transfers between devices with their start and end apart: 3, of which 0 were waited for; matrix products, arithmetic and copies ran while one was open for 0% of the time, Pallas kernels for 8%

profile of v4, /device:TPU:1, one launch (start us, length us, event | category | flops | bytes accessed | tf_op | source)
XLA Modules:
  0.0 104.1 jit_solution(15568098254459992357)
XLA Ops:
  0.6 3.6 %collective-permute-start = (bf16[256,1024]{1,0:T(8,128)(2,1)}, bf16[256,1024]{1,0:T(8,128)(2,1)S(1)}, u32[]{:S(2)}, u32[]{:S(2)}) collective-permute-start(bf16[256,1024]{1,0:T(8,128)(2,1)} %refs_0_.3), channel_id=1, source_target_pairs={{0,1},{1,2},{2,3},{3,0},{4,7},{5,4},{6,5},{7,6},{8,9},{9,10},{10,1... | collective-permute-start | bytes 1572872 | tf_op jit(solution)/shard_map/ppermute | solution.py:286
  4.3 0.0 copy-start.1
  4.3 0.0 copy-start.2
  4.3 7.9 %summary.1 = bf16[128,16,128]{2,1,0:T(8,128)(2,1)} custom-call(bf16[8192,1024]{1,0:T(8,128)(2,1)} %phi.5, bf16[8192,128]{1,0:T(8,128)(2,1)} %y.5, f32[1,256]{1,0:T(1,128)} %rates_away.1, f32[1,256]{1,0:T(1,128)} %bitcast.1), custom_call_target="tpu_custom_call" | custom-call | tf_op jit(solution)/shard_map/summary/pallas_call | solution.py:331
  12.2 0.0 copy-start
  12.2 0.0 collective-permute-done.refs_1_
  12.2 2.0 %collective-permute-start.2 = (bf16[256,1024]{1,0:T(8,128)(2,1)S(1)}, bf16[256,1024]{1,0:T(8,128)(2,1)S(1)}, u32[]{:S(2)}, u32[]{:S(2)}) collective-permute-start(bf16[256,1024]{1,0:T(8,128)(2,1)S(1)} %collective-permute-done.refs_1_), channel_id=1, source_target_pairs={{0,5},{1,6},{2,7},{3,4},{4,3},{5,0},{6,1},{7,2},{8,13},{9,14},{10,... | collective-permute-start | bytes 1572872 | tf_op jit(solution)/shard_map/ppermute | solution.py:286
  14.2 0.0 collective-permute-start.1
  14.2 22.4 %all_to_all.20.message = bf16[128,16,128]{2,1,0:T(8,128)(2,1)S(1)} all-to-all(bf16[128,16,128]{2,1,0:T(8,128)(2,1)} %summary.1), channel_id=1, replica_groups=mesh['region'=32,'basis'=4] {'region','basis'}, dimensions={0} | all-to-all | bytes 1048576 | tf_op jit(solution)/shard_map/all_to_all | solution.py:329
  36.7 0.0 collective-permute-done.2.refs_3_
  36.7 0.0 collective-permute-done.1.refs_2_
  36.7 0.0 copy-done.1
  36.7 0.0 copy-done.2
  36.7 1.7 %forward.1 = (bf16[128,8,128]{2,1,0:T(8,128)(2,1)S(1)}, f32[32,8,128]{2,1,0:T(8,128)S(1)}, f32[32,8,128]{2,1,0:T(8,128)S(1)}, f32[8,128]{1,0:T(8,128)S(1)}) custom-call(bf16[128,16,128]{2,1,0:T(8,128)(2,1)S(1)} %all_to_all.20.message, s32[8,8]{1,0:T(8,128)S(1)} %copy-done.2, bf16[256,1024]{1,0:T(8,128)(2,1)S(1)} %copy-done.1, ...), custom_call_target="tpu_custom_call" | custom-call | tf_op jit(solution)/shard_map/forward/pallas_call | solution.py:352
  38.4 14.7 %all_to_all.21.arrived = bf16[128,8,128]{2,1,0:T(8,128)(2,1)S(1)} all-to-all(bf16[128,8,128]{2,1,0:T(8,128)(2,1)S(1)} %get-tuple-element.12), channel_id=1, replica_groups=mesh['region'=32,'basis'=4] {'region','basis'}, dimensions={0} | all-to-all | bytes 524288 | tf_op jit(solution)/shard_map/all_to_all | solution.py:329
  53.0 0.0 copy-done
  53.0 9.1 %residual.1 = (bf16[128,8,128]{2,1,0:T(8,128)(2,1)S(1)}, bf16[128,1024]{1,0:T(8,128)(2,1)S(1)}) custom-call(bf16[8192,1024]{1,0:T(8,128)(2,1)} %phi.5, bf16[8192,128]{1,0:T(8,128)(2,1)S(1)} %copy-done, bf16[128,8,128]{2,1,0:T(8,128)(2,1)S(1)} %all_to_all.21.arrived), custom_call_target="tpu_custom_call" | custom-call | tf_op jit(solution)/shard_map/residual/pallas_call | solution.py:371
  62.1 15.0 %all_to_all.22.message = bf16[128,8,128]{2,1,0:T(8,128)(2,1)S(1)} all-to-all(bf16[128,8,128]{2,1,0:T(8,128)(2,1)S(1)} %get-tuple-element.14), channel_id=1, replica_groups=mesh['region'=32,'basis'=4] {'region','basis'}, dimensions={0} | all-to-all | bytes 524288 | tf_op jit(solution)/shard_map/all_to_all | solution.py:329
  77.1 1.3 %backward.1 = bf16[384,4,128]{2,1,0:T(4,128)(2,1)S(1)} custom-call(bf16[128,8,128]{2,1,0:T(8,128)(2,1)S(1)} %all_to_all.22.message, s32[8,8]{1,0:T(8,128)S(1)} %copy-done.2, f32[32,8,128]{2,1,0:T(8,128)S(1)} %get-tuple-element.15.previous, f32[32,8,128]{2,1,0:T(8,128)S(1)} %get-tuple-element.16.rates, f32[8,128]{1,0:T(8,128)S(1)} %get-tuple-element.17.loads, ...), custom_call_target="tpu_custom_call" | custom-call | tf_op jit(solution)/shard_map/backward/pallas_call | solution.py:387
  78.4 16.4 %all_to_all.23.arrived = bf16[384,4,128]{2,1,0:T(4,128)(2,1)S(1)} all-to-all(bf16[384,4,128]{2,1,0:T(4,128)(2,1)S(1)} %backward.1), channel_id=1, replica_groups=mesh['region'=32,'basis'=4] {'region','basis'}, dimensions={0} | all-to-all | bytes 786432 | tf_op jit(solution)/shard_map/all_to_all | solution.py:329
  94.8 9.1 %gradient.1 = (bf16[8192,128]{1,0:T(8,128)(2,1)}, f32[1,256]{1,0:T(1,128)}) custom-call(bf16[8192,1024]{1,0:T(8,128)(2,1)} %phi.5, bf16[8192,128]{1,0:T(8,128)(2,1)S(1)} %copy-done, bf16[128,1024]{1,0:T(8,128)(2,1)S(1)} %get-tuple-element.13.loaded, bf16[384,4,128]{2,1,0:T(4,128)(2,1)S(1)} %all_to_all.23.arrived), custom_call_target="tpu_custom_call" | custom-call | tf_op jit(solution)/shard_map/gradient/pallas_call | solution.py:397
Async XLA Ops:
  0.6 11.5 %collective-permute-start = (bf16[256,1024]{1,0:T(8,128)(2,1)}, bf16[256,1024]{1,0:T(8,128)(2,1)S(1)}, u32[]{:S(2)}, u32[]{:S(2)}) collective-permute-start(bf16[256,1024]{1,0:T(8,128)(2,1)} %refs_0_.3), channel_id=1, source_target_pairs={{0,1},{1,2},{2,3},{3,0},{4,7},{5,4},{6,5},{7,6},{8,9},{9,10},{10,1... | collective-permute-start | bytes 1572872 | tf_op jit(solution)/shard_map/ppermute | solution.py:286
  4.3 32.4 %copy-start.1 = (bf16[256,1024]{1,0:T(8,128)(2,1)S(1)}, bf16[256,1024]{1,0:T(8,128)(2,1)}, u32[]{:S(2)}) copy-start(bf16[256,1024]{1,0:T(8,128)(2,1)} %refs_0_.3) | copy-start | bytes 1572868
  4.3 32.4 %copy-start.2 = (s32[8,8]{1,0:T(8,128)S(1)}, s32[8,8]{1,0:T(8,128)}, u32[]{:S(2)}) copy-start(s32[8,8]{1,0:T(8,128)} %pattern.3) | copy-start | bytes 772
  12.2 40.9 %copy-start = (bf16[8192,128]{1,0:T(8,128)(2,1)S(1)}, bf16[8192,128]{1,0:T(8,128)(2,1)}, u32[]{:S(2)}) copy-start(bf16[8192,128]{1,0:T(8,128)(2,1)} %y.5) | copy-start | bytes 6291460
  12.2 24.5 %collective-permute-start.2 = (bf16[256,1024]{1,0:T(8,128)(2,1)S(1)}, bf16[256,1024]{1,0:T(8,128)(2,1)S(1)}, u32[]{:S(2)}, u32[]{:S(2)}) collective-permute-start(bf16[256,1024]{1,0:T(8,128)(2,1)S(1)} %collective-permute-done.refs_1_), channel_id=1, source_target_pairs={{0,5},{1,6},{2,7},{3,4},{4,3},{5,0},{6,1},{7,2},{8,13},{9,14},{10,... | collective-permute-start | bytes 1572872 | tf_op jit(solution)/shard_map/ppermute | solution.py:286
  14.2 22.5 %collective-permute-start.1 = (bf16[256,1024]{1,0:T(8,128)(2,1)S(1)}, bf16[256,1024]{1,0:T(8,128)(2,1)S(1)}, u32[]{:S(2)}, u32[]{:S(2)}) collective-permute-start(bf16[256,1024]{1,0:T(8,128)(2,1)S(1)} %collective-permute-done.refs_1_), channel_id=1, source_target_pairs={{0,4},{1,5},{2,6},{3,7},{4,0},{5,1},{6,2},{7,3},{8,12},{9,13},{10,... | collective-permute-start | bytes 1572872 | tf_op jit(solution)/shard_map/ppermute | solution.py:286

commit v5 on v4

--- a/solution.py
+++ b/solution.py
@@ -61,12 +61,16 @@
     return lax.dot_general(first, second, (((1,), (1,)), ((), ())), preferred_element_type=F32)
 
 
-def store_by_trait(total, spread, message):
+def scatter_traits(total, spread):
     traits, width = total.shape
     groups = width // LANES
     for s in range(groups):
         spread[pl.ds(s, traits, stride=groups), :] = total[:, s * LANES : (s + 1) * LANES]
-    message[:, 0:groups, :] = spread[...].reshape(traits, groups, LANES).astype(BF16)
+
+
+def store_by_trait(total, spread, message):
+    scatter_traits(total, spread)
+    message[...] = spread[...].reshape(message.shape).astype(BF16)
 
 
 def gather_traits(spread, target, traits, groups):
@@ -113,27 +117,31 @@
             total[...] = product
         else:
             total[...] += product
-    store_by_trait(total[...], spread, message)
+    scatter_traits(total[...], spread)
     wait_all(small)
-    groups = total.shape[1] // LANES
-    pieces = []
-    for vector in (rates, loads):
-        width = vector.shape[1] // LANES
-        parts = [split(vector[:, h * LANES : (h + 1) * LANES]) for h in range(width)]
-        pieces += [part[0] for part in parts] + [part[1] for part in parts]
-    tail = jnp.concatenate([piece.astype(F32) for piece in pieces], axis=0).astype(BF16)
-    message[:, groups : groups + tail.shape[0], :] = jnp.broadcast_to(
-        tail[None], (message.shape[0],) + tail.shape
-    )
+    traits, width = total.shape
+    groups = width // LANES
+    rows = [slice(h * LANES, (h + 1) * LANES) for h in range(rates.shape[1] // LANES)]
+    highs, lows = zip(*[split(rates[:, at]) for at in rows])
+    first = lax.axis_index("region") == 0
+    lows = [jnp.where(first, loads[:, at], low.astype(F32)) for at, low in zip(rows, lows)]
+    tail = jnp.concatenate([high.astype(F32) for high in highs] + lows, axis=0).astype(BF16)
+    for k in range(traits):
+        for part in range(PARTS - 1):
+            at = k * groups + part * PART_ROWS
+            message[k * PARTS + part] = spread[at : at + PART_ROWS, :].astype(BF16)
+        message[k * PARTS + PARTS - 1] = tail
 
 
 def forward_kernel(count, message, pattern, *refs):
     *pieces, reply, previous, rates, loads, sums, wide, tiles = refs
-    devices, rows, _ = message.shape
+    rows = PARTS * PART_ROWS
+    devices = message.shape[0] // PARTS
     owners = devices // count
     groups = pieces[0].shape[1] // LANES
     halves = groups // owners
-    wide[...] = message[...].astype(F32).reshape(devices * rows, LANES)
+    for i in range(devices * PARTS):
+        wide[i * PART_ROWS : (i + 1) * PART_ROWS, :] = message[i].astype(F32)
     step = owners * rows
 
     def column(row):
@@ -146,17 +154,15 @@
             block = block + column(b * rows + s)
         summary.append(block.astype(BF16).astype(F32))
         sums[s] = summary[s]
+    later = lax.broadcasted_iota(jnp.int32, (count, LANES), 0) > 0
+    load_rows = []
     for b in range(owners):
         for h in range(halves):
             at = b * rows + groups + h
-            rates_block = column(at) + column(at + halves)
-            tiles[pl.ds(b * halves + h, count, stride=groups), :] = rates_block
+            low = jnp.where(later, column(at + halves), 0.0)
+            tiles[pl.ds(b * halves + h, count, stride=groups), :] = column(at) + low
+            load_rows.append(wide[at + halves : at + halves + 1, :])
     rates[...] = tiles[...].reshape(count, groups, LANES)
-    load_rows = []
-    for b in range(owners):
-        for h in range(halves):
-            at = b * rows + groups + 2 * halves + h
-            load_rows.append(wide[at : at + 1, :] + wide[at + halves : at + halves + 1, :])
     loads[...] = jnp.concatenate(load_rows, axis=0)
     for piece, s in zip(pieces, piece_blocks()):
         kept = [keep(summary, [pattern[t, k] for k in range(groups)]) for t in (s, s + 1)]
@@ -317,7 +323,7 @@
     spread = pltpu.VMEM((traits * groups, LANES), F32)
     tiles = pltpu.VMEM((count * groups, LANES), F32)
     short = jax.ShapeDtypeStruct((devices, groups, LANES), BF16)
-    long = jax.ShapeDtypeStruct((devices, 2 * groups, LANES), BF16)
+    long = jax.ShapeDtypeStruct((devices * PARTS, PART_ROWS, LANES), BF16)
 
     def sems(*shape):
         return pltpu.SemaphoreType.DMA(shape)
@@ -361,7 +367,7 @@
         ),
         scratch_shapes=[
             pltpu.VMEM((groups, count, LANES), F32),
-            pltpu.VMEM((devices * 2 * groups, LANES), F32),
+            pltpu.VMEM((devices * PARTS * PART_ROWS, LANES), F32),
             tiles,
         ],
         compiler_params=limit(16),
@@ -388,7 +394,7 @@
         functools.partial(backward_kernel, count, traits),
         in_specs=[vmem, smem, vmem, vmem, vmem] + [vmem] * len(pieces),
         out_specs=vmem,
-        out_shape=jax.ShapeDtypeStruct((devices * PARTS, PART_ROWS, LANES), BF16),
+        out_shape=long,
         scratch_shapes=[tiles],
         compiler_params=limit(16),
         name="backward",

time: 104 us -> 103 us (level)
  blocking collectives: 68.5 us -> 67.3 us
    all_to_all x4, blocking collectives: 68.5 us -> 67.3 us  [exchange(): return lax.all_to_all(value, ALL, 0, 0, tiled=True)]
where the time goes in v5:
time: 103 us
  blocking collectives  67.3 us (65%)
  Pallas kernels  28.9 us (28%)
  starting transfers between devices  5.67 us (6%)
    all_to_all x4, blocking collectives, exchange(): return lax.all_to_all(value, ALL, 0, 0, tiled=True)  67.3 us
    pallas_call x1, Pallas kernels, shards(): pl.pallas_call(functools.partial(gradient_kernel, tapered, halves), in_sp...  9.12 us
    pallas_call x1, Pallas kernels, shards(): pl.pallas_call(functools.partial(residual_kernel, even), in_specs=[hbm, v...  9.08 us
    pallas_call x1, Pallas kernels, shards(): pl.pallas_call(functools.partial(summary_kernel, tapered), in_specs=[hbm]...  7.88 us
    ppermute x3, starting transfers between devices, permute(): return lax.ppermute(value, ALL, pairs)  5.67 us
  transfers between devices with their start and end apart: 3, of which 0 were waited for; matrix products, arithmetic and copies ran while one was open for 0% of the time, Pallas kernels for 8%

profile of v5, /device:TPU:1, one launch (start us, length us, event | category | flops | bytes accessed | tf_op | source)
XLA Modules:
  0.0 102.8 jit_solution(11384669464486457170)
XLA Ops:
  0.6 3.6 %collective-permute-start = (bf16[256,1024]{1,0:T(8,128)(2,1)}, bf16[256,1024]{1,0:T(8,128)(2,1)S(1)}, u32[]{:S(2)}, u32[]{:S(2)}) collective-permute-start(bf16[256,1024]{1,0:T(8,128)(2,1)} %refs_0_.3), channel_id=1, source_target_pairs={{0,1},{1,2},{2,3},{3,0},{4,7},{5,4},{6,5},{7,6},{8,9},{9,10},{10,1... | collective-permute-start | bytes 1572872 | tf_op jit(solution)/shard_map/ppermute | solution.py:292
  4.3 0.0 copy-start.1
  4.3 0.0 copy-start.2
  4.3 7.9 %summary.1 = bf16[384,4,128]{2,1,0:T(4,128)(2,1)} custom-call(bf16[8192,1024]{1,0:T(8,128)(2,1)} %phi.5, bf16[8192,128]{1,0:T(8,128)(2,1)} %y.5, f32[1,256]{1,0:T(1,128)} %rates_away.1, f32[1,256]{1,0:T(1,128)} %bitcast.1), custom_call_target="tpu_custom_call" | custom-call | tf_op jit(solution)/shard_map/summary/pallas_call | solution.py:337
  12.2 0.0 copy-start
  12.2 0.0 collective-permute-done.refs_1_
  12.2 2.0 %collective-permute-start.2 = (bf16[256,1024]{1,0:T(8,128)(2,1)S(1)}, bf16[256,1024]{1,0:T(8,128)(2,1)S(1)}, u32[]{:S(2)}, u32[]{:S(2)}) collective-permute-start(bf16[256,1024]{1,0:T(8,128)(2,1)S(1)} %collective-permute-done.refs_1_), channel_id=1, source_target_pairs={{0,5},{1,6},{2,7},{3,4},{4,3},{5,0},{6,1},{7,2},{8,13},{9,14},{10,... | collective-permute-start | bytes 1572872 | tf_op jit(solution)/shard_map/ppermute | solution.py:292
  14.2 0.0 collective-permute-start.1
  14.2 21.0 %all_to_all.20.message = bf16[384,4,128]{2,1,0:T(4,128)(2,1)S(1)} all-to-all(bf16[384,4,128]{2,1,0:T(4,128)(2,1)} %summary.1), channel_id=1, replica_groups=mesh['region'=32,'basis'=4] {'region','basis'}, dimensions={0} | all-to-all | bytes 786432 | tf_op jit(solution)/shard_map/all_to_all | solution.py:335
  35.3 0.0 collective-permute-done.2.refs_3_
  35.3 0.0 collective-permute-done.1.refs_2_
  35.3 0.0 copy-done.1
  35.3 0.0 copy-done.2
  35.3 1.5 %forward.1 = (bf16[128,8,128]{2,1,0:T(8,128)(2,1)S(1)}, f32[32,8,128]{2,1,0:T(8,128)S(1)}, f32[32,8,128]{2,1,0:T(8,128)S(1)}, f32[8,128]{1,0:T(8,128)S(1)}) custom-call(bf16[384,4,128]{2,1,0:T(4,128)(2,1)S(1)} %all_to_all.20.message, s32[8,8]{1,0:T(8,128)S(1)} %copy-done.2, bf16[256,1024]{1,0:T(8,128)(2,1)S(1)} %copy-done.1, ...), custom_call_target="tpu_custom_call" | custom-call | tf_op jit(solution)/shard_map/forward/pallas_call | solution.py:358
  36.8 14.9 %all_to_all.21.arrived = bf16[128,8,128]{2,1,0:T(8,128)(2,1)S(1)} all-to-all(bf16[128,8,128]{2,1,0:T(8,128)(2,1)S(1)} %get-tuple-element.12), channel_id=1, replica_groups=mesh['region'=32,'basis'=4] {'region','basis'}, dimensions={0} | all-to-all | bytes 524288 | tf_op jit(solution)/shard_map/all_to_all | solution.py:335
  51.7 0.0 copy-done
  51.7 9.1 %residual.1 = (bf16[128,8,128]{2,1,0:T(8,128)(2,1)S(1)}, bf16[128,1024]{1,0:T(8,128)(2,1)S(1)}) custom-call(bf16[8192,1024]{1,0:T(8,128)(2,1)} %phi.5, bf16[8192,128]{1,0:T(8,128)(2,1)S(1)} %copy-done, bf16[128,8,128]{2,1,0:T(8,128)(2,1)S(1)} %all_to_all.21.arrived), custom_call_target="tpu_custom_call" | custom-call | tf_op jit(solution)/shard_map/residual/pallas_call | solution.py:377
  60.8 15.0 %all_to_all.22.message = bf16[128,8,128]{2,1,0:T(8,128)(2,1)S(1)} all-to-all(bf16[128,8,128]{2,1,0:T(8,128)(2,1)S(1)} %get-tuple-element.14), channel_id=1, replica_groups=mesh['region'=32,'basis'=4] {'region','basis'}, dimensions={0} | all-to-all | bytes 524288 | tf_op jit(solution)/shard_map/all_to_all | solution.py:335
  75.8 1.3 %backward.1 = bf16[384,4,128]{2,1,0:T(4,128)(2,1)S(1)} custom-call(bf16[128,8,128]{2,1,0:T(8,128)(2,1)S(1)} %all_to_all.22.message, s32[8,8]{1,0:T(8,128)S(1)} %copy-done.2, f32[32,8,128]{2,1,0:T(8,128)S(1)} %get-tuple-element.15.previous, f32[32,8,128]{2,1,0:T(8,128)S(1)} %get-tuple-element.16.rates, f32[8,128]{1,0:T(8,128)S(1)} %get-tuple-element.17.loads, ...), custom_call_target="tpu_custom_call" | custom-call | tf_op jit(solution)/shard_map/backward/pallas_call | solution.py:393
  77.1 16.4 %all_to_all.23.arrived = bf16[384,4,128]{2,1,0:T(4,128)(2,1)S(1)} all-to-all(bf16[384,4,128]{2,1,0:T(4,128)(2,1)S(1)} %backward.1), channel_id=1, replica_groups=mesh['region'=32,'basis'=4] {'region','basis'}, dimensions={0} | all-to-all | bytes 786432 | tf_op jit(solution)/shard_map/all_to_all | solution.py:335
  93.5 9.1 %gradient.1 = (bf16[8192,128]{1,0:T(8,128)(2,1)}, f32[1,256]{1,0:T(1,128)}) custom-call(bf16[8192,1024]{1,0:T(8,128)(2,1)} %phi.5, bf16[8192,128]{1,0:T(8,128)(2,1)S(1)} %copy-done, bf16[128,1024]{1,0:T(8,128)(2,1)S(1)} %get-tuple-element.13.loaded, bf16[384,4,128]{2,1,0:T(4,128)(2,1)S(1)} %all_to_all.23.arrived), custom_call_target="tpu_custom_call" | custom-call | tf_op jit(solution)/shard_map/gradient/pallas_call | solution.py:403
Async XLA Ops:
  0.6 11.5 %collective-permute-start = (bf16[256,1024]{1,0:T(8,128)(2,1)}, bf16[256,1024]{1,0:T(8,128)(2,1)S(1)}, u32[]{:S(2)}, u32[]{:S(2)}) collective-permute-start(bf16[256,1024]{1,0:T(8,128)(2,1)} %refs_0_.3), channel_id=1, source_target_pairs={{0,1},{1,2},{2,3},{3,0},{4,7},{5,4},{6,5},{7,6},{8,9},{9,10},{10,1... | collective-permute-start | bytes 1572872 | tf_op jit(solution)/shard_map/ppermute | solution.py:292
  4.3 31.0 %copy-start.1 = (bf16[256,1024]{1,0:T(8,128)(2,1)S(1)}, bf16[256,1024]{1,0:T(8,128)(2,1)}, u32[]{:S(2)}) copy-start(bf16[256,1024]{1,0:T(8,128)(2,1)} %refs_0_.3) | copy-start | bytes 1572868
  4.3 31.0 %copy-start.2 = (s32[8,8]{1,0:T(8,128)S(1)}, s32[8,8]{1,0:T(8,128)}, u32[]{:S(2)}) copy-start(s32[8,8]{1,0:T(8,128)} %pattern.3) | copy-start | bytes 772
  12.2 39.5 %copy-start = (bf16[8192,128]{1,0:T(8,128)(2,1)S(1)}, bf16[8192,128]{1,0:T(8,128)(2,1)}, u32[]{:S(2)}) copy-start(bf16[8192,128]{1,0:T(8,128)(2,1)} %y.5) | copy-start | bytes 6291460
  12.2 23.1 %collective-permute-start.2 = (bf16[256,1024]{1,0:T(8,128)(2,1)S(1)}, bf16[256,1024]{1,0:T(8,128)(2,1)S(1)}, u32[]{:S(2)}, u32[]{:S(2)}) collective-permute-start(bf16[256,1024]{1,0:T(8,128)(2,1)S(1)} %collective-permute-done.refs_1_), channel_id=1, source_target_pairs={{0,5},{1,6},{2,7},{3,4},{4,3},{5,0},{6,1},{7,2},{8,13},{9,14},{10,... | collective-permute-start | bytes 1572872 | tf_op jit(solution)/shard_map/ppermute | solution.py:292
  14.2 21.1 %collective-permute-start.1 = (bf16[256,1024]{1,0:T(8,128)(2,1)S(1)}, bf16[256,1024]{1,0:T(8,128)(2,1)S(1)}, u32[]{:S(2)}, u32[]{:S(2)}) collective-permute-start(bf16[256,1024]{1,0:T(8,128)(2,1)S(1)} %collective-permute-done.refs_1_), channel_id=1, source_target_pairs={{0,4},{1,5},{2,6},{3,7},{4,0},{5,1},{6,2},{7,3},{8,12},{9,13},{10,... | collective-permute-start | bytes 1572872 | tf_op jit(solution)/shard_map/ppermute | solution.py:292

commit v6 on v5

--- a/solution.py
+++ b/solution.py
@@ -179,16 +179,18 @@
             reply[r * owners + b] = value
 
 
-def residual_kernel(sizes, phi, y, arrived, message, kept, phi_here, weights, total, spread, sems):
+def residual_kernel(
+    sizes, phi, y, arrived, message, residuals, phi_here, weights, total, spread, sems
+):
     chunks = start_chunks(sizes, ((phi, phi_here),), sems)
     traits = arrived.shape[0]
     load_by_trait(arrived, spread, weights)
     weights[traits:, :] = weights[:traits, :]
-    kept[...] = weights[:traits, :]
     for i, (at, copies) in enumerate(chunks):
         wait_all(copies)
         fitted = contract_lanes(weights[...], phi_here[at, :])[:traits]
         residual = (fitted - y[at, :].T.astype(F32)).astype(BF16)
+        residuals[:, at] = residual
         product = jnp.dot(residual, phi_here[at, :], preferred_element_type=F32)
         if i == 0:
             total[...] = product
@@ -248,30 +250,29 @@
 
 
 def gradient_kernel(
-    sizes, halves, phi, y, loaded, arrived, out, slope, phi_here, out_here, weights, spread, sent, sems
+    sizes, halves, phi, residuals, arrived, out, slope, phi_here, out_here, weights, spread, sent, sems
 ):
     chunks = start_chunks(sizes, ((phi, phi_here),), sems)
-    traits = loaded.shape[0]
+    traits = residuals.shape[0]
     groups = weights.shape[1] // LANES
     for k in range(traits):
         for part in range(PARTS - 1):
             at = k * groups + part * PART_ROWS
             spread[at : at + PART_ROWS, :] = arrived[k * PARTS + part].astype(F32)
     gather_traits(spread, weights, traits, groups)
-    weights[traits:, :] = loaded[...]
+    weights[traits:, :] = weights[:traits, :]
     stores = []
 
     def finish(i):
         at = chunks[i][0]
-        both = sent[i % 2, :, 0 : sizes[i]]
-        residual = (both[traits:] - y[at, :].T.astype(F32)).astype(BF16)
-        out_here[at, :] = (both[:traits] - residual.astype(F32)).astype(BF16).T
+        back = sent[i % 2, :, 0 : sizes[i]]
+        out_here[at, :] = (back - residuals[:, at].astype(F32)).astype(BF16).T
         stores.append(pltpu.make_async_copy(out_here.at[at], out.at[at], sems.at[1, i]))
         stores[-1].start()
 
     for i, (at, copies) in enumerate(chunks):
         wait_all(copies)
-        sent[i % 2, :, 0 : sizes[i]] = contract_lanes(weights[...], phi_here[at, :])
+        sent[i % 2, :, 0 : sizes[i]] = contract_lanes(weights[...], phi_here[at, :])[:traits]
         if i > 0:
             finish(i - 1)
     finish(len(chunks) - 1)
@@ -311,7 +312,7 @@
     halves = share // LANES
     tile = min(TILE_ROWS, rows)
     even = (tile,) * (rows // tile)
-    tapered = (tile // 2,) * 2 + even[2:] + (tile // 2,) * 2
+    tapered = (tile // 2,) * 2 + even[2:] + (tile // 2, tile // 4, tile // 4)
     near = near_shard(mixing)
 
     hbm = pl.BlockSpec(memory_space=pl.ANY)
@@ -374,11 +375,11 @@
         name="forward",
     )(sums, pattern, *pieces)
     loaded = exchange(loaded)
-    pulled, loaded = pl.pallas_call(
+    pulled, residuals = pl.pallas_call(
         functools.partial(residual_kernel, even),
         in_specs=[hbm, vmem, vmem],
         out_specs=(vmem, vmem),
-        out_shape=(short, jax.ShapeDtypeStruct((traits, width), BF16)),
+        out_shape=(short, jax.ShapeDtypeStruct((traits, rows), BF16)),
         scratch_shapes=[
             phi_here,
             pltpu.VMEM((2 * traits, width), BF16),
@@ -402,7 +403,7 @@
     back = exchange(back)
     obs_grad, slope = pl.pallas_call(
         functools.partial(gradient_kernel, tapered, halves),
-        in_specs=[hbm, vmem, vmem, vmem],
+        in_specs=[hbm, vmem, vmem],
         out_specs=(hbm, vmem),
         out_shape=(
             jax.ShapeDtypeStruct((rows, traits), BF16),
@@ -413,12 +414,12 @@
             y_here,
             pltpu.VMEM((2 * traits, width), BF16),
             spread,
-            pltpu.VMEM((2, 2 * traits, tile), F32),
+            pltpu.VMEM((2, traits, tile), F32),
             sems(2, len(tapered)),
         ],
         compiler_params=limit(44),
         name="gradient",
-    )(basis_values, observations, loaded, back)
+    )(basis_values, residuals, back)
     return obs_grad, slope
 
 

time: 103 us -> 103 us (level)
  no operation moved by 1% of the time
where the time goes in v6:
time: 103 us
  blocking collectives  67.4 us (65%)
  Pallas kernels  29.3 us (28%)
  starting transfers between devices  5.61 us (5%)
    all_to_all x4, blocking collectives, exchange(): return lax.all_to_all(value, ALL, 0, 0, tiled=True)  67.4 us
    pallas_call x1, Pallas kernels, shards(): pl.pallas_call(functools.partial(gradient_kernel, tapered, halves), in_sp...  9.5 us
    pallas_call x1, Pallas kernels, shards(): pl.pallas_call(functools.partial(residual_kernel, even), in_specs=[hbm, v...  9.08 us
    pallas_call x1, Pallas kernels, shards(): pl.pallas_call(functools.partial(summary_kernel, tapered), in_specs=[hbm]...  7.94 us
    ppermute x3, starting transfers between devices, permute(): return lax.ppermute(value, ALL, pairs)  5.61 us
  transfers between devices with their start and end apart: 3, of which 0 were waited for; matrix products, arithmetic and copies ran while one was open for 0% of the time, Pallas kernels for 8%

profile of v6, /device:TPU:1, one launch (start us, length us, event | category | flops | bytes accessed | tf_op | source)
XLA Modules:
  0.0 103.2 jit_solution(5663051615471197672)
XLA Ops:
  0.6 3.6 %collective-permute-start = (bf16[256,1024]{1,0:T(8,128)(2,1)}, bf16[256,1024]{1,0:T(8,128)(2,1)S(1)}, u32[]{:S(2)}, u32[]{:S(2)}) collective-permute-start(bf16[256,1024]{1,0:T(8,128)(2,1)} %refs_0_.3), channel_id=1, source_target_pairs={{0,1},{1,2},{2,3},{3,0},{4,7},{5,4},{6,5},{7,6},{8,9},{9,10},{10,1... | collective-permute-start | bytes 1572872 | tf_op jit(solution)/shard_map/ppermute | solution.py:293
  4.3 0.0 copy-start.1
  4.3 0.0 copy-start.2
  4.3 7.9 %summary.1 = bf16[384,4,128]{2,1,0:T(4,128)(2,1)} custom-call(bf16[8192,1024]{1,0:T(8,128)(2,1)} %phi.5, bf16[8192,128]{1,0:T(8,128)(2,1)} %y.3, f32[1,256]{1,0:T(1,128)} %rates_away.1, f32[1,256]{1,0:T(1,128)} %bitcast.1), custom_call_target="tpu_custom_call" | custom-call | tf_op jit(solution)/shard_map/summary/pallas_call | solution.py:338
  12.2 0.0 copy-start
  12.2 0.0 collective-permute-done.refs_1_
  12.2 2.0 %collective-permute-start.2 = (bf16[256,1024]{1,0:T(8,128)(2,1)S(1)}, bf16[256,1024]{1,0:T(8,128)(2,1)S(1)}, u32[]{:S(2)}, u32[]{:S(2)}) collective-permute-start(bf16[256,1024]{1,0:T(8,128)(2,1)S(1)} %collective-permute-done.refs_1_), channel_id=1, source_target_pairs={{0,5},{1,6},{2,7},{3,4},{4,3},{5,0},{6,1},{7,2},{8,13},{9,14},{10,... | collective-permute-start | bytes 1572872 | tf_op jit(solution)/shard_map/ppermute | solution.py:293
  14.2 0.0 collective-permute-start.1
  14.2 21.1 %all_to_all.20.message = bf16[384,4,128]{2,1,0:T(4,128)(2,1)S(1)} all-to-all(bf16[384,4,128]{2,1,0:T(4,128)(2,1)} %summary.1), channel_id=1, replica_groups=mesh['region'=32,'basis'=4] {'region','basis'}, dimensions={0} | all-to-all | bytes 786432 | tf_op jit(solution)/shard_map/all_to_all | solution.py:336
  35.3 0.0 collective-permute-done.2.refs_3_
  35.3 0.0 collective-permute-done.1.refs_2_
  35.3 0.0 copy-done.1
  35.3 0.0 copy-done.2
  35.3 1.5 %forward.1 = (bf16[128,8,128]{2,1,0:T(8,128)(2,1)S(1)}, f32[32,8,128]{2,1,0:T(8,128)S(1)}, f32[32,8,128]{2,1,0:T(8,128)S(1)}, f32[8,128]{1,0:T(8,128)S(1)}) custom-call(bf16[384,4,128]{2,1,0:T(4,128)(2,1)S(1)} %all_to_all.20.message, s32[8,8]{1,0:T(8,128)S(1)} %copy-done.2, bf16[256,1024]{1,0:T(8,128)(2,1)S(1)} %copy-done.1, ...), custom_call_target="tpu_custom_call" | custom-call | tf_op jit(solution)/shard_map/forward/pallas_call | solution.py:359
  36.9 14.8 %all_to_all.21.arrived = bf16[128,8,128]{2,1,0:T(8,128)(2,1)S(1)} all-to-all(bf16[128,8,128]{2,1,0:T(8,128)(2,1)S(1)} %get-tuple-element.12), channel_id=1, replica_groups=mesh['region'=32,'basis'=4] {'region','basis'}, dimensions={0} | all-to-all | bytes 524288 | tf_op jit(solution)/shard_map/all_to_all | solution.py:336
  51.7 0.0 copy-done
  51.8 9.1 %residual.1 = (bf16[128,8,128]{2,1,0:T(8,128)(2,1)S(1)}, bf16[128,8192]{1,0:T(8,128)(2,1)S(1)}) custom-call(bf16[8192,1024]{1,0:T(8,128)(2,1)} %phi.5, bf16[8192,128]{1,0:T(8,128)(2,1)S(1)} %copy-done, bf16[128,8,128]{2,1,0:T(8,128)(2,1)S(1)} %all_to_all.21.arrived), custom_call_target="tpu_custom_call" | custom-call | tf_op jit(solution)/shard_map/residual/pallas_call | solution.py:378
  60.8 15.0 %all_to_all.22.message = bf16[128,8,128]{2,1,0:T(8,128)(2,1)S(1)} all-to-all(bf16[128,8,128]{2,1,0:T(8,128)(2,1)S(1)} %get-tuple-element.14), channel_id=1, replica_groups=mesh['region'=32,'basis'=4] {'region','basis'}, dimensions={0} | all-to-all | bytes 524288 | tf_op jit(solution)/shard_map/all_to_all | solution.py:336
  75.8 1.3 %backward.1 = bf16[384,4,128]{2,1,0:T(4,128)(2,1)S(1)} custom-call(bf16[128,8,128]{2,1,0:T(8,128)(2,1)S(1)} %all_to_all.22.message, s32[8,8]{1,0:T(8,128)S(1)} %copy-done.2, f32[32,8,128]{2,1,0:T(8,128)S(1)} %get-tuple-element.15.previous, f32[32,8,128]{2,1,0:T(8,128)S(1)} %get-tuple-element.16.rates, f32[8,128]{1,0:T(8,128)S(1)} %get-tuple-element.17.loads, ...), custom_call_target="tpu_custom_call" | custom-call | tf_op jit(solution)/shard_map/backward/pallas_call | solution.py:394
  77.1 16.4 %all_to_all.23.arrived = bf16[384,4,128]{2,1,0:T(4,128)(2,1)S(1)} all-to-all(bf16[384,4,128]{2,1,0:T(4,128)(2,1)S(1)} %backward.1), channel_id=1, replica_groups=mesh['region'=32,'basis'=4] {'region','basis'}, dimensions={0} | all-to-all | bytes 786432 | tf_op jit(solution)/shard_map/all_to_all | solution.py:336
  93.5 9.5 %gradient.1 = (bf16[8192,128]{1,0:T(8,128)(2,1)}, f32[1,256]{1,0:T(1,128)}) custom-call(bf16[8192,1024]{1,0:T(8,128)(2,1)} %phi.5, bf16[128,8192]{1,0:T(8,128)(2,1)S(1)} %get-tuple-element.13.residuals, bf16[384,4,128]{2,1,0:T(4,128)(2,1)S(1)} %all_to_all.23.arrived), custom_call_target="tpu_custom_call" | custom-call | tf_op jit(solution)/shard_map/gradient/pallas_call | solution.py:404
Async XLA Ops:
  0.6 11.6 %collective-permute-start = (bf16[256,1024]{1,0:T(8,128)(2,1)}, bf16[256,1024]{1,0:T(8,128)(2,1)S(1)}, u32[]{:S(2)}, u32[]{:S(2)}) collective-permute-start(bf16[256,1024]{1,0:T(8,128)(2,1)} %refs_0_.3), channel_id=1, source_target_pairs={{0,1},{1,2},{2,3},{3,0},{4,7},{5,4},{6,5},{7,6},{8,9},{9,10},{10,1... | collective-permute-start | bytes 1572872 | tf_op jit(solution)/shard_map/ppermute | solution.py:293
  4.3 31.1 %copy-start.1 = (bf16[256,1024]{1,0:T(8,128)(2,1)S(1)}, bf16[256,1024]{1,0:T(8,128)(2,1)}, u32[]{:S(2)}) copy-start(bf16[256,1024]{1,0:T(8,128)(2,1)} %refs_0_.3) | copy-start | bytes 1572868
  4.3 31.1 %copy-start.2 = (s32[8,8]{1,0:T(8,128)S(1)}, s32[8,8]{1,0:T(8,128)}, u32[]{:S(2)}) copy-start(s32[8,8]{1,0:T(8,128)} %pattern.3) | copy-start | bytes 772
  12.2 39.5 %copy-start = (bf16[8192,128]{1,0:T(8,128)(2,1)S(1)}, bf16[8192,128]{1,0:T(8,128)(2,1)}, u32[]{:S(2)}) copy-start(bf16[8192,128]{1,0:T(8,128)(2,1)} %y.3) | copy-start | bytes 6291460
  12.2 23.1 %collective-permute-start.2 = (bf16[256,1024]{1,0:T(8,128)(2,1)S(1)}, bf16[256,1024]{1,0:T(8,128)(2,1)S(1)}, u32[]{:S(2)}, u32[]{:S(2)}) collective-permute-start(bf16[256,1024]{1,0:T(8,128)(2,1)S(1)} %collective-permute-done.refs_1_), channel_id=1, source_target_pairs={{0,5},{1,6},{2,7},{3,4},{4,3},{5,0},{6,1},{7,2},{8,13},{9,14},{10,... | collective-permute-start | bytes 1572872 | tf_op jit(solution)/shard_map/ppermute | solution.py:293
  14.2 21.1 %collective-permute-start.1 = (bf16[256,1024]{1,0:T(8,128)(2,1)S(1)}, bf16[256,1024]{1,0:T(8,128)(2,1)S(1)}, u32[]{:S(2)}, u32[]{:S(2)}) collective-permute-start(bf16[256,1024]{1,0:T(8,128)(2,1)S(1)} %collective-permute-done.refs_1_), channel_id=1, source_target_pairs={{0,4},{1,5},{2,6},{3,7},{4,0},{5,1},{6,2},{7,3},{8,12},{9,13},{10,... | collective-permute-start | bytes 1572872 | tf_op jit(solution)/shard_map/ppermute | solution.py:293

commit v7 on v6

--- a/solution.py
+++ b/solution.py
@@ -312,7 +312,7 @@
     halves = share // LANES
     tile = min(TILE_ROWS, rows)
     even = (tile,) * (rows // tile)
-    tapered = (tile // 2,) * 2 + even[2:] + (tile // 2, tile // 4, tile // 4)
+    tapered = (tile // 2,) * 2 + even[2:] + (tile // 2,) * 2
     near = near_shard(mixing)
 
     hbm = pl.BlockSpec(memory_space=pl.ANY)

time: 103 us -> 103 us (level)
  no operation moved by 1% of the time
where the time goes in v7:
time: 103 us
  blocking collectives  67.3 us (65%)
  Pallas kernels  28.9 us (28%)
  starting transfers between devices  5.67 us (6%)
    all_to_all x4, blocking collectives, exchange(): return lax.all_to_all(value, ALL, 0, 0, tiled=True)  67.3 us
    pallas_call x1, Pallas kernels, shards(): pl.pallas_call(functools.partial(gradient_kernel, tapered, halves), in_sp...  9.1 us
    pallas_call x1, Pallas kernels, shards(): pl.pallas_call(functools.partial(residual_kernel, even), in_specs=[hbm, v...  9.08 us
    pallas_call x1, Pallas kernels, shards(): pl.pallas_call(functools.partial(summary_kernel, tapered), in_specs=[hbm]...  7.88 us
    ppermute x3, starting transfers between devices, permute(): return lax.ppermute(value, ALL, pairs)  5.67 us
  transfers between devices with their start and end apart: 3, of which 0 were waited for; matrix products, arithmetic and copies ran while one was open for 0% of the time, Pallas kernels for 8%

profile of v7, /device:TPU:1, one launch (start us, length us, event | category | flops | bytes accessed | tf_op | source)
XLA Modules:
  0.0 102.7 jit_solution(4428701881536991712)
XLA Ops:
  0.6 3.6 %collective-permute-start = (bf16[256,1024]{1,0:T(8,128)(2,1)}, bf16[256,1024]{1,0:T(8,128)(2,1)S(1)}, u32[]{:S(2)}, u32[]{:S(2)}) collective-permute-start(bf16[256,1024]{1,0:T(8,128)(2,1)} %refs_0_.3), channel_id=1, source_target_pairs={{0,1},{1,2},{2,3},{3,0},{4,7},{5,4},{6,5},{7,6},{8,9},{9,10},{10,1... | collective-permute-start | bytes 1572872 | tf_op jit(solution)/shard_map/ppermute | solution.py:293
  4.3 0.0 copy-start.1
  4.3 0.0 copy-start.2
  4.3 7.9 %summary.1 = bf16[384,4,128]{2,1,0:T(4,128)(2,1)} custom-call(bf16[8192,1024]{1,0:T(8,128)(2,1)} %phi.5, bf16[8192,128]{1,0:T(8,128)(2,1)} %y.3, f32[1,256]{1,0:T(1,128)} %rates_away.1, f32[1,256]{1,0:T(1,128)} %bitcast.1), custom_call_target="tpu_custom_call" | custom-call | tf_op jit(solution)/shard_map/summary/pallas_call | solution.py:338
  12.2 0.0 copy-start
  12.2 0.0 collective-permute-done.refs_1_
  12.2 2.0 %collective-permute-start.2 = (bf16[256,1024]{1,0:T(8,128)(2,1)S(1)}, bf16[256,1024]{1,0:T(8,128)(2,1)S(1)}, u32[]{:S(2)}, u32[]{:S(2)}) collective-permute-start(bf16[256,1024]{1,0:T(8,128)(2,1)S(1)} %collective-permute-done.refs_1_), channel_id=1, source_target_pairs={{0,5},{1,6},{2,7},{3,4},{4,3},{5,0},{6,1},{7,2},{8,13},{9,14},{10,... | collective-permute-start | bytes 1572872 | tf_op jit(solution)/shard_map/ppermute | solution.py:293
  14.2 0.0 collective-permute-start.1
  14.2 21.0 %all_to_all.20.message = bf16[384,4,128]{2,1,0:T(4,128)(2,1)S(1)} all-to-all(bf16[384,4,128]{2,1,0:T(4,128)(2,1)} %summary.1), channel_id=1, replica_groups=mesh['region'=32,'basis'=4] {'region','basis'}, dimensions={0} | all-to-all | bytes 786432 | tf_op jit(solution)/shard_map/all_to_all | solution.py:336
  35.3 0.0 collective-permute-done.2.refs_3_
  35.3 0.0 collective-permute-done.1.refs_2_
  35.3 0.0 copy-done.1
  35.3 0.0 copy-done.2
  35.3 1.5 %forward.1 = (bf16[128,8,128]{2,1,0:T(8,128)(2,1)S(1)}, f32[32,8,128]{2,1,0:T(8,128)S(1)}, f32[32,8,128]{2,1,0:T(8,128)S(1)}, f32[8,128]{1,0:T(8,128)S(1)}) custom-call(bf16[384,4,128]{2,1,0:T(4,128)(2,1)S(1)} %all_to_all.20.message, s32[8,8]{1,0:T(8,128)S(1)} %copy-done.2, bf16[256,1024]{1,0:T(8,128)(2,1)S(1)} %copy-done.1, ...), custom_call_target="tpu_custom_call" | custom-call | tf_op jit(solution)/shard_map/forward/pallas_call | solution.py:359
  36.8 14.9 %all_to_all.21.arrived = bf16[128,8,128]{2,1,0:T(8,128)(2,1)S(1)} all-to-all(bf16[128,8,128]{2,1,0:T(8,128)(2,1)S(1)} %get-tuple-element.12), channel_id=1, replica_groups=mesh['region'=32,'basis'=4] {'region','basis'}, dimensions={0} | all-to-all | bytes 524288 | tf_op jit(solution)/shard_map/all_to_all | solution.py:336
  51.7 0.0 copy-done
  51.7 9.1 %residual.1 = (bf16[128,8,128]{2,1,0:T(8,128)(2,1)S(1)}, bf16[128,8192]{1,0:T(8,128)(2,1)S(1)}) custom-call(bf16[8192,1024]{1,0:T(8,128)(2,1)} %phi.5, bf16[8192,128]{1,0:T(8,128)(2,1)S(1)} %copy-done, bf16[128,8,128]{2,1,0:T(8,128)(2,1)S(1)} %all_to_all.21.arrived), custom_call_target="tpu_custom_call" | custom-call | tf_op jit(solution)/shard_map/residual/pallas_call | solution.py:378
  60.8 15.0 %all_to_all.22.message = bf16[128,8,128]{2,1,0:T(8,128)(2,1)S(1)} all-to-all(bf16[128,8,128]{2,1,0:T(8,128)(2,1)S(1)} %get-tuple-element.14), channel_id=1, replica_groups=mesh['region'=32,'basis'=4] {'region','basis'}, dimensions={0} | all-to-all | bytes 524288 | tf_op jit(solution)/shard_map/all_to_all | solution.py:336
  75.8 1.3 %backward.1 = bf16[384,4,128]{2,1,0:T(4,128)(2,1)S(1)} custom-call(bf16[128,8,128]{2,1,0:T(8,128)(2,1)S(1)} %all_to_all.22.message, s32[8,8]{1,0:T(8,128)S(1)} %copy-done.2, f32[32,8,128]{2,1,0:T(8,128)S(1)} %get-tuple-element.15.previous, f32[32,8,128]{2,1,0:T(8,128)S(1)} %get-tuple-element.16.rates, f32[8,128]{1,0:T(8,128)S(1)} %get-tuple-element.17.loads, ...), custom_call_target="tpu_custom_call" | custom-call | tf_op jit(solution)/shard_map/backward/pallas_call | solution.py:394
  77.1 16.4 %all_to_all.23.arrived = bf16[384,4,128]{2,1,0:T(4,128)(2,1)S(1)} all-to-all(bf16[384,4,128]{2,1,0:T(4,128)(2,1)S(1)} %backward.1), channel_id=1, replica_groups=mesh['region'=32,'basis'=4] {'region','basis'}, dimensions={0} | all-to-all | bytes 786432 | tf_op jit(solution)/shard_map/all_to_all | solution.py:336
  93.5 9.1 %gradient.1 = (bf16[8192,128]{1,0:T(8,128)(2,1)}, f32[1,256]{1,0:T(1,128)}) custom-call(bf16[8192,1024]{1,0:T(8,128)(2,1)} %phi.5, bf16[128,8192]{1,0:T(8,128)(2,1)S(1)} %get-tuple-element.13.residuals, bf16[384,4,128]{2,1,0:T(4,128)(2,1)S(1)} %all_to_all.23.arrived), custom_call_target="tpu_custom_call" | custom-call | tf_op jit(solution)/shard_map/gradient/pallas_call | solution.py:404
Async XLA Ops:
  0.6 11.5 %collective-permute-start = (bf16[256,1024]{1,0:T(8,128)(2,1)}, bf16[256,1024]{1,0:T(8,128)(2,1)S(1)}, u32[]{:S(2)}, u32[]{:S(2)}) collective-permute-start(bf16[256,1024]{1,0:T(8,128)(2,1)} %refs_0_.3), channel_id=1, source_target_pairs={{0,1},{1,2},{2,3},{3,0},{4,7},{5,4},{6,5},{7,6},{8,9},{9,10},{10,1... | collective-permute-start | bytes 1572872 | tf_op jit(solution)/shard_map/ppermute | solution.py:293
  4.3 31.0 %copy-start.1 = (bf16[256,1024]{1,0:T(8,128)(2,1)S(1)}, bf16[256,1024]{1,0:T(8,128)(2,1)}, u32[]{:S(2)}) copy-start(bf16[256,1024]{1,0:T(8,128)(2,1)} %refs_0_.3) | copy-start | bytes 1572868
  4.3 31.0 %copy-start.2 = (s32[8,8]{1,0:T(8,128)S(1)}, s32[8,8]{1,0:T(8,128)}, u32[]{:S(2)}) copy-start(s32[8,8]{1,0:T(8,128)} %pattern.3) | copy-start | bytes 772
  12.2 39.5 %copy-start = (bf16[8192,128]{1,0:T(8,128)(2,1)S(1)}, bf16[8192,128]{1,0:T(8,128)(2,1)}, u32[]{:S(2)}) copy-start(bf16[8192,128]{1,0:T(8,128)(2,1)} %y.3) | copy-start | bytes 6291460
  12.2 23.1 %collective-permute-start.2 = (bf16[256,1024]{1,0:T(8,128)(2,1)S(1)}, bf16[256,1024]{1,0:T(8,128)(2,1)S(1)}, u32[]{:S(2)}, u32[]{:S(2)}) collective-permute-start(bf16[256,1024]{1,0:T(8,128)(2,1)S(1)} %collective-permute-done.refs_1_), channel_id=1, source_target_pairs={{0,5},{1,6},{2,7},{3,4},{4,3},{5,0},{6,1},{7,2},{8,13},{9,14},{10,... | collective-permute-start | bytes 1572872 | tf_op jit(solution)/shard_map/ppermute | solution.py:293
  14.2 21.1 %collective-permute-start.1 = (bf16[256,1024]{1,0:T(8,128)(2,1)S(1)}, bf16[256,1024]{1,0:T(8,128)(2,1)S(1)}, u32[]{:S(2)}, u32[]{:S(2)}) collective-permute-start(bf16[256,1024]{1,0:T(8,128)(2,1)S(1)} %collective-permute-done.refs_1_), channel_id=1, source_target_pairs={{0,4},{1,5},{2,6},{3,7},{4,0},{5,1},{6,2},{7,3},{8,12},{9,13},{10,... | collective-permute-start | bytes 1572872 | tf_op jit(solution)/shard_map/ppermute | solution.py:293
